TPU v7x, 32 devices: a whole 2x2x4 slice. The times are simulated.
32 devices in a mesh: seq: 16 (over z, x, core), tp: 2 (over y).
Axes of the slice: x: 2, y: 2, z: 4, core: 2. Of those that a mesh axis runs over, the one named last changes fastest.
Arguments:
- tokens: bfloat16 [8192, 4096], P('seq'), may hold values from -6 to 6
- w_in: bfloat16 [4096, 3, 4096], P('seq', None, 'tp'), may hold values from -0.09375 to 0.09375
- short_taps: float32 [3, 3, 4096], P(None, None, 'tp'), may hold values from -3 to 3
- decay_rate: float32 [256, 16], P('tp'), may hold values from 1.2207031e-05 to 0.04, as said below
- residue: float32 [256, 16], P('tp'), may hold values from -4 to 4
- skip_gain: float32 [4096], P('tp'), may hold values from -4 to 4
- w_out: bfloat16 [4096, 4096], P('tp'), may hold values from -0.125 to 0.125
Outputs:
- mixed: bfloat16 [8192, 4096], P('seq', 'tp')
Inputs may be any that keep to these rules, and one draw needn't show every extreme that they name: `decay_rate`: every decay rate is positive.
All inputs are finite; a program needn't handle non-finite values.
Results may differ from a plain program's by a relative error of at most 0.0075.
Values may be sent and summed in bfloat16 or wider, within the bound.
A program may use at most 192 MiB of HBM per device.

v0:
```python
import functools

import jax
import jax.numpy as jnp
from jax import lax
from jax.experimental import pallas as pl
from jax.experimental.pallas import tpu as pltpu
from jax.sharding import PartitionSpec as P

SUB = 128
LANES = 256
HALO = 16
MESH = pl.DeviceIdType.MESH
HIGHEST = lax.Precision.HIGHEST


def shifted_by(block, axis, distance):
    devices = range(lax.axis_size(axis))
    route = [(i - distance, i) for i in devices if i - distance in devices]
    return lax.ppermute(block, axis, route)


def fanned(state, width, order):
    lanes = state.shape[1]
    tile = lanes // width
    full = jnp.concatenate([state] * tile, axis=0)
    row = lax.broadcasted_iota(jnp.int32, full.shape, 0) // order
    lane = lax.broadcasted_iota(jnp.int32, full.shape, 1) // width
    return jnp.where(row == lane, full, 0.0)


def split(value):
    high = value.astype(jnp.bfloat16)
    return high, (value - high.astype(jnp.float32)).astype(jnp.bfloat16)


def product3(a, b):
    (ah, al), (bh, bl) = split(a), split(b)
    dot = functools.partial(jnp.dot, preferred_element_type=jnp.float32)
    return dot(ah, bh) + (dot(ah, bl) + dot(al, bh))


def conv_kernel(
    width, q_ref, k_ref, v_ref, taps_ref, lags_ref, leave_ref, reach_ref, fade_ref, skip_ref,
    query_ref, base_ref, state_ref, toep_ref
):
    taps = taps_ref.shape[0]
    count, lanes = query_ref.shape
    order = state_ref.shape[0]
    tile = lanes // width

    def filtered(ref, which):
        value = ref[...].astype(jnp.float32)
        total = None
        for tap in range(taps):
            term = taps_ref[tap, which][None, :] * value[HALO - tap : HALO - tap + count]
            total = term if total is None else total + term
        return total

    query_ref[...] = filtered(q_ref, 0)
    gated = filtered(k_ref, 1) * filtered(v_ref, 2)
    lane = lax.broadcasted_iota(jnp.int32, (SUB, lanes), 1) // width
    row = lax.broadcasted_iota(jnp.int32, (tile * order, lanes), 0) // order
    diagonal = row == lax.broadcasted_iota(jnp.int32, (tile * order, lanes), 1) // width

    @pl.when(pl.program_id(1) == 0)
    def _():
        below = lax.broadcasted_iota(jnp.int32, (SUB, SUB), 0) >= lax.broadcasted_iota(
            jnp.int32, (SUB, SUB), 1
        )
        for g in range(tile):
            wide = jnp.broadcast_to(lags_ref[g : g + 1], (SUB, SUB))
            rolled = pltpu.roll(wide, 0, 1, stride=1, stride_axis=0)
            toep_ref[g * SUB : (g + 1) * SUB] = jnp.where(below, rolled, 0.0).astype(jnp.bfloat16)

    toep = toep_ref[...]
    state = jnp.zeros((tile * order, lanes), jnp.float32)
    for block in range(count // SUB):
        piece = gated[block * SUB : (block + 1) * SUB]
        wide = jnp.dot(toep, piece.astype(jnp.bfloat16), preferred_element_type=jnp.float32)
        local = skip_ref[...] * piece
        picked = wide[:SUB]
        for g in range(1, tile):
            picked = jnp.where(lane == g, wide[g * SUB : (g + 1) * SUB], picked)
        local = local + picked
        if block:
            local = local + product3(reach_ref[:SUB], state)
        base_ref[block * SUB : (block + 1) * SUB] = local
        fresh = product3(leave_ref[...], piece)
        state = fade_ref[...] * state + jnp.where(diagonal, fresh, 0.0)
    compact = state[:order]
    for g in range(1, tile):
        compact = compact + state[g * order : (g + 1) * order]
    state_ref[...] = compact


def convolved(proj, taps, lags, leave, reach, fade, skip, width, order, count):
    chans = skip.shape[1]
    lanes = min(LANES, chans)
    steps = chans // lanes
    tile = lanes // width
    segments, rows, _ = proj.shape
    return pl.pallas_call(
        functools.partial(conv_kernel, width),
        grid=(steps, segments),
        in_specs=[
            pl.BlockSpec((None, rows, lanes), lambda i, j: (j, 0, i)),
            pl.BlockSpec((None, rows, lanes), lambda i, j: (j, 0, steps + i)),
            pl.BlockSpec((None, rows, lanes), lambda i, j: (j, 0, 2 * steps + i)),
            pl.BlockSpec((taps.shape[0], 3, lanes), lambda i, j: (0, 0, i)),
            pl.BlockSpec((tile, SUB), lambda i, j: (i, 0)),
            pl.BlockSpec((tile * order, SUB), lambda i, j: (i, 0)),
            pl.BlockSpec((count, tile * order), lambda i, j: (0, i)),
            pl.BlockSpec((tile * order, 1), lambda i, j: (i, 0)),
            pl.BlockSpec((1, lanes), lambda i, j: (0, i)),
        ],
        out_specs=[
            pl.BlockSpec((None, count, lanes), lambda i, j: (j, 0, i)),
            pl.BlockSpec((None, count, lanes), lambda i, j: (j, 0, i)),
            pl.BlockSpec((None, order, lanes), lambda i, j: (j, 0, i)),
        ],
        out_shape=[
            jax.ShapeDtypeStruct((segments, count, chans), jnp.float32),
            jax.ShapeDtypeStruct((segments, count, chans), jnp.float32),
            jax.ShapeDtypeStruct((segments, order, chans), jnp.float32),
        ],
        scratch_shapes=[pltpu.VMEM((tile * SUB, SUB), jnp.bfloat16)],
        cost_estimate=pl.CostEstimate(
            flops=2 * count * chans * SUB * tile, bytes_accessed=count * chans * 20, transcendentals=0
        ),
        name="conv",
    )(proj, proj, proj, taps, lags, leave, reach, fade, skip)


def place():
    size, here = lax.axis_size("seq"), lax.axis_index("seq")
    return here // 4, lax.rem(here // 2, 2), lax.rem(here, 2), size // 4


def index_of(z, x, core):
    return z * 4 + x * 2 + core


def greet(peers):
    barrier = pltpu.get_barrier_semaphore()
    for peer in peers:
        pl.semaphore_signal(barrier, inc=1, device_id=peer, device_id_type=MESH)
    pl.semaphore_wait(barrier, len(peers))


def remote(source, target, send_sem, recv_sem, peer):
    return pltpu.make_async_remote_copy(
        src_ref=source,
        dst_ref=target,
        send_sem=send_sem,
        recv_sem=recv_sem,
        device_id=peer,
        device_id_type=MESH,
    )


def gather_kernel(
    own_ref, halo_ref, pieces_ref, out_ref, tok_ref, w_ref, wo_ref, held_ref, held_w_ref, local_sems,
    line_send, line_recv, pass_send, pass_recv, pair_send, pair_recv,
    tp_send, tp_recv, core_send, core_recv, early_send, early_recv,
    cols_send, cols_recv, swap_send, swap_recv, halo_send, halo_recv,
):
    z, x, core, depth = place()
    parity = lax.rem(z, 2)
    n_tp, part = lax.axis_size("tp"), lax.axis_index("tp")
    mine = index_of(z, x, core)
    side = {"seq": index_of(z, 1 - x, core)}
    twin = {"seq": index_of(z, x, 1 - core)}

    def on_line(hop):
        there = z ^ hop[0]
        return there, (1 - core if hop[1] else core)

    hops = [(step, other) for step in range(depth) for other in range(2)][1:]
    peers = [side] + [
        {"seq": index_of(there, x, which)} for there, which in map(on_line, hops)
    ]
    tps = [{"tp": lax.rem(part + d, n_tp)} for d in range(1, n_tp)]
    greet(peers + tps)

    cols = own_ref.shape[1] // (2 * n_tp)

    def band(which, piece):
        return pl.ds(pl.multiple_of((2 * which + piece) * cols, cols), cols)

    own_slot, mate_slot = 2 * parity + core, 2 * (1 - parity) + core
    body = pl.ds(HALO, own_ref.shape[0])
    head = pl.ds(0, HALO)
    taken = [
        pltpu.make_async_copy(own_ref, held_ref.at[body], local_sems.at[0]),
        pltpu.make_async_copy(halo_ref, held_ref.at[head], local_sems.at[1]),
        pltpu.make_async_copy(pieces_ref.at[own_slot], held_w_ref, local_sems.at[2]),
    ]
    stay = [
        pltpu.make_async_copy(held_ref, tok_ref.at[own_slot], local_sems.at[3]),
        pltpu.make_async_copy(held_w_ref, w_ref.at[mine], local_sems.at[4]),
    ]
    for copy in taken:
        copy.start()
    started = []

    def begin(*what):
        copy = remote(*what)
        copy.start()
        started.append(copy)
        return copy

    def to_line(hop):
        there, which = on_line(hop)
        index = 2 * hop[0] + hop[1]
        return begin(
            pieces_ref.at[2 * lax.rem(there, 2) + which], w_ref.at[mine],
            line_send.at[index], line_recv.at[index], {"seq": index_of(there, x, which)},
        )

    def to_pair(piece):
        where = tok_ref.at[own_slot, body, band(part, piece)]
        return begin(
            own_ref.at[:, band(part, piece)], where, pair_send.at[piece], pair_recv.at[piece],
            {"seq": index_of(z ^ 1, x, core)},
        )

    quarter = wo_ref.shape[1] // 4
    out_cols = wo_ref.shape[2]

    def quarter_rows(piece):
        return pl.ds(pl.multiple_of((2 * core + piece) * quarter, quarter), quarter)

    def columns(d, piece):
        target = lax.rem(part + d, n_tp)
        slot = 2 * (d - 1) + piece
        return begin(
            out_ref.at[quarter_rows(piece), pl.ds(pl.multiple_of(target * out_cols, out_cols), out_cols)],
            wo_ref.at[d - 1, quarter_rows(piece)],
            cols_send.at[slot], cols_recv.at[slot], tps[d - 1],
        )

    def swap(d, piece):
        slot = 2 * (d - 1) + piece
        where = wo_ref.at[d - 1, quarter_rows(piece)]
        return begin(where, where, swap_send.at[slot], swap_recv.at[slot], twin)

    paired = [to_pair(0)]
    first = begin(
        pieces_ref.at[own_slot], w_ref.at[mine], pass_send.at[0], pass_recv.at[0], side
    )
    line = {}
    for hop in hops[:2]:
        line[hop] = to_line(hop)
    paired.append(to_pair(1))
    for hop in hops[2:]:
        line[hop] = to_line(hop)
    moved = {(d, 0): columns(d, 0) for d in range(1, n_tp)}
    early = begin(own_ref, tok_ref.at[own_slot, body], early_send, early_recv, twin)
    heads = []
    for n, hop in enumerate(hops[:3]):
        there, which = on_line(hop)
        heads.append(begin(
            halo_ref, tok_ref.at[own_slot, head], halo_send.at[n], halo_recv.at[n],
            {"seq": index_of(there, x, which)},
        ))
    for copy in taken:
        copy.wait()
    for copy in stay:
        copy.start()

    forwards = []

    def hand_on(hop):
        index = 2 * hop[0] + hop[1]
        source = index_of(on_line(hop)[0], x, on_line(hop)[1])
        line[hop].wait_recv()
        forwards.append(begin(
            w_ref.at[source], w_ref.at[source], pass_send.at[index], pass_recv.at[index], side
        ))

    twins, across = [], {}

    def to_twin(which, piece, d):
        where = tok_ref.at[mate_slot, body, band(which, piece)]
        slot = 2 * d + piece
        twins.append(begin(where, where, core_send.at[slot], core_recv.at[slot], twin))

    def pair_on(piece):
        paired[piece].wait_recv()
        where = tok_ref.at[mate_slot, body, band(part, piece)]
        for d in range(1, n_tp):
            slot = 2 * (d - 1) + piece
            across[d, piece] = begin(
                where, where, tp_send.at[slot], tp_recv.at[slot], tps[d - 1]
            )
        to_twin(part, piece, 0)

    hand_on(hops[0])
    pair_on(0)
    hand_on(hops[1])
    hand_on(hops[3])
    pair_on(1)
    for d in range(1, n_tp):
        moved[d, 1] = columns(d, 1)
    hand_on(hops[2])
    for hop in hops[4:]:
        hand_on(hop)
    for piece in range(2):
        for d in range(1, n_tp):
            moved[d, piece].wait_recv()
            twins.append(swap(d, piece))
            across[d, piece].wait_recv()
            to_twin(lax.rem(part - d + n_tp, n_tp), piece, d)
    for copy in [first, early] + heads + forwards + twins:
        copy.wait_recv()
    for copy in started:
        copy.wait_send()
    for copy in stay:
        copy.wait()


def gathered(own, halo, pieces, w_out):
    size, n_tp = lax.axis_size("seq"), lax.axis_size("tp")
    line = size // 2
    anywhere = pl.BlockSpec(memory_space=pl.ANY)
    counts = [5, line, line, line, line, 2, 2] + [2 * n_tp] * 4 + [0, 0] + [2 * n_tp] * 4 + [3, 3]
    return pl.pallas_call(
        gather_kernel,
        out_shape=[
            jax.ShapeDtypeStruct((4, HALO + own.shape[0], own.shape[1]), own.dtype),
            jax.ShapeDtypeStruct((size,) + pieces.shape[1:], pieces.dtype),
            jax.ShapeDtypeStruct(
                (n_tp - 1, w_out.shape[0], w_out.shape[1] // n_tp), w_out.dtype
            ),
        ],
        in_specs=[anywhere] * 4,
        out_specs=[anywhere] * 3,
        scratch_shapes=[
            pltpu.VMEM((HALO + own.shape[0], own.shape[1]), own.dtype),
            pltpu.VMEM(pieces.shape[1:], pieces.dtype),
        ]
        + [pltpu.SemaphoreType.DMA((n,) if n else ()) for n in counts],
        compiler_params=pltpu.CompilerParams(collective_id=0, has_side_effects=True),
        name="gather",
    )(own, halo, pieces, w_out)


def share_kernel(own_ref, all_ref, send_sems, recv_sems):
    total = all_ref.shape[0]
    z, x, core, depth = place()
    here = (z // 2) * 2 + x

    def peer(d):
        there = lax.rem(here + d, total)
        return {"seq": index_of(2 * (there // 2) + lax.rem(z, 2), lax.rem(there, 2), core)}

    peers = [peer(d) for d in range(1, total)]
    greet(peers)
    copies = []
    for d in range(1, total):
        copy = remote(
            own_ref, all_ref.at[here], send_sems.at[d - 1], recv_sems.at[d - 1], peers[d - 1]
        )
        copy.start()
        copies.append(copy)
    all_ref[here] = own_ref[...]
    for copy in copies:
        copy.wait()


def shared(state):
    total = lax.axis_size("seq") // 4
    return pl.pallas_call(
        share_kernel,
        out_shape=jax.ShapeDtypeStruct((total,) + state.shape, state.dtype),
        in_specs=[pl.BlockSpec(memory_space=pltpu.VMEM)],
        out_specs=pl.BlockSpec(memory_space=pltpu.VMEM),
        scratch_shapes=[
            pltpu.SemaphoreType.DMA((total - 1,)),
            pltpu.SemaphoreType.DMA((total - 1,)),
        ],
        compiler_params=pltpu.CompilerParams(collective_id=1, has_side_effects=True),
        name="share",
    )(state)


def spread_kernel(mix_ref, full_ref, local_sem, send_sems, recv_sems, tp_send, tp_recv):
    z, x, core, _ = place()
    chans = mix_ref.shape[2]
    n_tp, part = lax.axis_size("tp"), lax.axis_index("tp")
    parity = lax.rem(z, 2)
    me = 2 * parity + core

    def peer(d):
        there = (z ^ (d // 2), (1 - core if d % 2 else core))
        return 2 * lax.rem(there[0], 2) + there[1], {"seq": index_of(there[0], x, there[1])}

    tps = [{"tp": lax.rem(part + d, n_tp)} for d in range(1, n_tp)]
    greet([peer(d)[1] for d in range(1, 4)] + tps)

    def at(slot, which):
        return full_ref.at[slot, :, pl.ds(pl.multiple_of(which * chans, chans), chans)]

    across = []

    def over(source, which, n):
        for d in range(1, n_tp):
            sem = 4 * (d - 1) + n
            copy = remote(source, at(d, which), tp_send.at[sem], tp_recv.at[sem], tps[d - 1])
            copy.start()
            across.append(copy)

    copies = []
    for d in (2, 3, 1):
        there, device = peer(d)
        copy = remote(
            mix_ref.at[there], at(0, me), send_sems.at[d - 1], recv_sems.at[d - 1], device
        )
        copy.start()
        copies.append((d, copy))
    over(mix_ref.at[me], me, 0)
    stay = pltpu.make_async_copy(mix_ref.at[me], at(0, me), local_sem)
    stay.start()
    for d, copy in copies[2:] + copies[:2]:
        copy.wait_recv()
        which = peer(d)[0]
        over(at(0, which), which, d)
    for _, copy in copies:
        copy.wait_send()
    for copy in across:
        copy.wait()
    stay.wait()


def spread(mix):
    n_tp = lax.axis_size("tp")
    roles, count, chans = mix.shape
    return pl.pallas_call(
        spread_kernel,
        out_shape=jax.ShapeDtypeStruct((n_tp, count, roles * chans), mix.dtype),
        in_specs=[pl.BlockSpec(memory_space=pltpu.VMEM)],
        out_specs=pl.BlockSpec(memory_space=pltpu.VMEM),
        scratch_shapes=[
            pltpu.SemaphoreType.DMA(()),
            pltpu.SemaphoreType.DMA((3,)),
            pltpu.SemaphoreType.DMA((3,)),
            pltpu.SemaphoreType.DMA((4 * n_tp,)),
            pltpu.SemaphoreType.DMA((4 * n_tp,)),
        ],
        compiler_params=pltpu.CompilerParams(collective_id=2, has_side_effects=True),
        name="spread",
    )(mix)


def mix_kernel(width, query_ref, base_ref, all_ref, weight_ref, reach_ref, mix_ref):
    order = all_ref.shape[1]
    entering = jnp.sum(all_ref[...] * weight_ref[...], axis=0)
    carried = product3(reach_ref[...], fanned(entering, width, order))
    mix_ref[...] = (query_ref[...] * (base_ref[...] + carried)).astype(mix_ref.dtype)


def mixed_of(query, base, everything, weight, reach, width):
    segments, count, chans = query.shape
    size, order, _ = everything.shape
    lanes = min(LANES, chans)
    cols = lanes // width * order
    return pl.pallas_call(
        functools.partial(mix_kernel, width),
        grid=(chans // lanes, segments),
        in_specs=[
            pl.BlockSpec((None, count, lanes), lambda i, j: (j, 0, i)),
            pl.BlockSpec((None, count, lanes), lambda i, j: (j, 0, i)),
            pl.BlockSpec((size, order, lanes), lambda i, j: (0, 0, i)),
            pl.BlockSpec((None, size, order, lanes), lambda i, j: (j, 0, 0, i)),
            pl.BlockSpec((count, cols), lambda i, j: (0, i)),
        ],
        out_specs=pl.BlockSpec((None, count, lanes), lambda i, j: (j, 0, i)),
        out_shape=jax.ShapeDtypeStruct((segments, count, chans), jnp.bfloat16),
        name="mix",
    )(query, base, everything, weight, reach)


def shards(tokens, w_in, short_taps, decay_rate, residue, skip_gain, w_out):
    count = tokens.shape[0]
    rows, _, all_chans = w_in.shape
    width = all_chans // decay_rate.shape[0]
    taps = short_taps.shape[0]
    z, x, core, depth = place()
    parity = lax.rem(z, 2)
    role = 2 * parity + core
    n_tp, part = lax.axis_size("tp"), lax.axis_index("tp")
    chans = all_chans // 4

    before = shifted_by(tokens[count - (taps - 1) :], "seq", 1)
    halo = jnp.pad(before, ((HALO - (taps - 1), 0), (0, 0)))
    pieces = w_in.reshape(rows, 3, 4, chans).transpose(2, 0, 1, 3).reshape(4, rows, 3 * chans)
    tok, weights, out_rows = gathered(tokens, halo, pieces, w_out)

    def own(array, axis):
        share = array.shape[axis] // 4
        return lax.dynamic_slice_in_dim(array, role * share, share, axis)

    short_taps, skip = own(short_taps, 2), own(skip_gain[None], 1)
    decay_rate, residue = own(decay_rate, 0), own(residue, 0)
    groups, order = decay_rate.shape
    weight_mode = residue * jnp.sqrt(2.0 * decay_rate / order)
    offsets = jnp.arange(SUB, dtype=jnp.float32)
    back = (-jnp.arange(SUB) % SUB).astype(jnp.float32)
    lags = jnp.einsum(
        "gm,gmd->gd",
        weight_mode,
        jnp.exp(-decay_rate[:, :, None] * back[None, None, :]),
        precision=HIGHEST,
    )
    rate = decay_rate.reshape(groups * order)
    leave = jnp.exp(-rate[:, None] * (SUB - 1.0 - offsets[None, :]))
    fade = jnp.exp(-rate * SUB)[:, None]
    positions = jnp.arange(count, dtype=jnp.float32)
    reach = weight_mode.reshape(groups * order)[None] * jnp.exp(
        -rate[None] * (positions[:, None] + 1.0)
    )
    by_mode = jnp.repeat(decay_rate.T, width, axis=1)
    slot = jnp.arange(4)
    own_block = index_of(2 * (z // 2) + slot // 2, x, slot % 2)
    team = jnp.arange(depth)[:, None]
    other_block = index_of(2 * (team // 2) + slot[None] // 2, team % 2, slot[None] % 2).reshape(-1)
    ahead = (own_block[:, None] - 1 - other_block[None, :])[:, :, None, None]
    weight = jnp.where(
        ahead >= 0, jnp.exp(-by_mode * (count * jnp.maximum(ahead, 0).astype(jnp.float32))), 0.0
    )

    proj = jnp.dot(
        tok.reshape(-1, tok.shape[2]),
        weights.reshape(-1, weights.shape[2]),
        preferred_element_type=jnp.float32,
    ).astype(jnp.bfloat16).reshape(4, -1, 3 * chans)
    query, base, final = convolved(
        proj, short_taps, lags, leave, reach, fade, skip, width, order, count
    )
    everything = shared(final).reshape(-1, order, chans)
    full = spread(mixed_of(query, base, everything, weight, reach, width))

    share = w_out.shape[1] // n_tp
    kept = lax.dynamic_slice_in_dim(w_out, part * share, share, axis=1)
    total = jnp.dot(full[0], kept, preferred_element_type=jnp.float32)
    for d in range(1, n_tp):
        total = total + jnp.dot(full[d], out_rows[d - 1], preferred_element_type=jnp.float32)
    return total.astype(jnp.bfloat16)


def solution(mesh):
    in_specs = (
        P("seq", None),
        P("seq", None, "tp"),
        P(None, None, "tp"),
        P("tp", None),
        P("tp", None),
        P("tp"),
        P("tp", None),
    )
    out_specs = P("seq", "tp")
    return jax.shard_map(shards, mesh=mesh, in_specs=in_specs, out_specs=out_specs, check_vma=False)
```

profile of v0, /device:TPU:0, one launch (start us, length us, event | category | flops | bytes accessed | tf_op | source)
XLA Modules:
  0.0 373.3 jit_solution(15840179019738800598)
XLA Ops:
  0.0 1.6 slice.9
  1.6 3.0 collective-permute-start
  4.6 0.6 fusion.19
  5.2 0.5 iota_subtract_fusion
  5.7 0.6 iota_add_fusion
  6.5 0.7 fusion.16
  7.2 0.6 subtract_compare_fusion
  7.8 1.4 multiply_exponential_fusion.1
  9.3 0.7 copy.25
  10.0 0.7 neg.48
  10.7 0.7 mul.153
  11.4 0.1 broadcast_in_dim.11
  11.5 0.2 neg.50
  11.6 1.8 fusion.10
  13.4 1.5 multiply_exponential_fusion.leave_ref
  14.9 1.9 exponential_multiply_fusion.reach_ref
  16.8 2.4 exponential_select_fusion.weight_ref
  19.2 0.6 constant_dynamic-slice_fusion.taps_ref
  19.8 2.8 copy.17
  22.6 2.1 copy.18
  24.7 2.8 copy.19.pieces_ref
  27.6 0.9 exp.31.fade_ref
  28.5 1.3 dynamic-slice.3
  29.8 1.4 pad.4.halo_ref
  31.2 188.8 %gather.1 = (bf16[4,528,4096]{2,1,0:T(8,128)(2,1)}, bf16[16,256,1536]{2,1,0:T(8,128)(2,1)}, bf16[1,2048,2048]{2,1,0:T(8,128)(2,1)}) custom-call(bf16[512,4096]{1,0:T(8,128)(2,1)} %own_ref.1, bf16[16,4096]{1,0:T(8,128)(2,1)} %pad.4.halo_ref, bf16[4,256,1536]{2,1,0:T(8,128)(2,1)} %copy.19.pieces_ref, bf16[2048,4096]{1,0:T(8,128)(2,1)} %out_ref.1), custom_call_target="tpu_custom_call" | custom-call | tf_op jit(solution)/shard_map/gather/pallas_call | solution.py:328
  220.0 34.5 %convolution_convert_fusion = bf16[2112,1536]{1,0:T(8,128)(2,1)} fusion(bf16[2112,4096]{1,0:T(8,128)(2,1)} %bitcast.37, bf16[4096,1536]{1,0:T(8,128)(2,1)} %bitcast.38), kind=kOutput, calls=%fused_computation | convolution fusion | flops 26578354176 | bytes 36372480 | tf_op jit(solution)/shard_map/dot_general | solution.py:533
  254.5 25.3 %conv.1 = (f32[4,512,512]{2,1,0:T(8,128)}, f32[4,512,512]{2,1,0:T(8,128)}, f32[4,16,512]{2,1,0:T(8,128)}) custom-call(bf16[4,528,1536]{2,1,0:T(8,128)(2,1)} %bitcast.27, bf16[4,528,1536]{2,1,0:T(8,128)(2,1)} %bitcast.28, bf16[4,528,1536]{2,1,0:T(8,128)(2,1)} %bitcast.29, f32[3,3,512]{2,1,0:T(4,128)} %constant_dynamic-slice_fusion.taps_ref, ...), custom_call_target="tpu_custom_call" | custom-call | flops 1073741824 | bytes 5242880 | tf_op jit(solution)/shard_map/conv/pallas_call | solution.py:103
  279.8 16.0 %share.1 = f32[4,4,16,512]{3,2,1,0:T(8,128)} custom-call(f32[4,16,512]{2,1,0:T(8,128)} %get-tuple-element.15.own_ref), custom_call_target="tpu_custom_call" | custom-call | tf_op jit(solution)/shard_map/share/pallas_call | solution.py:374
  295.8 9.2 %mix.1.mix_ref = bf16[4,512,512]{2,1,0:T(8,128)(2,1)} custom-call(f32[4,512,512]{2,1,0:T(8,128)} %get-tuple-element.13.query_ref, f32[4,512,512]{2,1,0:T(8,128)} %get-tuple-element.14.base_ref, f32[16,16,512]{2,1,0:T(8,128)} %bitcast.32, f32[4,16,16,512]{3,2,1,0:T(8,128)} %exponential_select_fusion.weight_ref, f32[512,512]{1,0:T(8,128)} %exponential_multiply_fusion.reach_ref), custom_call_target="tpu_custom_call" | custom-call | tf_op jit(solution)/shard_map/mix/pallas_call | solution.py:468
  305.1 51.3 %spread.1 = bf16[2,512,2048]{2,1,0:T(8,128)(2,1)} custom-call(bf16[4,512,512]{2,1,0:T(8,128)(2,1)} %mix.1.mix_ref), custom_call_target="tpu_custom_call" | custom-call | tf_op jit(solution)/shard_map/spread/pallas_call | solution.py:439
  356.4 7.7 %fusion.2 = f32[512,2048]{1,0:T(8,128)S(1)} fusion(bf16[2048,4096]{1,0:T(8,128)(2,1)} %out_ref.1, s32[]{:T(128)S(6)} %select_n.100, bf16[2,512,2048]{2,1,0:T(8,128)(2,1)} %spread.1), kind=kOutput, calls=%fused_computation.3 | convolution fusion | flops 4294967296 | bytes 14680068 | tf_op jit(solution)/shard_map/dot_general | solution.py:546
  364.1 9.2 %add_convert_fusion = bf16[512,2048]{1,0:T(8,128)(2,1)} fusion(f32[512,2048]{1,0:T(8,128)S(1)} %fusion.2, bf16[1,2048,2048]{2,1,0:T(8,128)(2,1)} %get-tuple-element.16, bf16[2,512,2048]{2,1,0:T(8,128)(2,1)S(1)} %copy-done.2), kind=kOutput, calls=%fused_computation.5 | convolution fusion | flops 4297064448 | bytes 16777216 | tf_op jit(solution)/shard_map/dot_general | solution.py:548
  (19 shorter events, 0.4 us)
Async XLA Ops:
  0.0 19.2 %copy-start = (f32[3,3,2048]{2,1,0:T(4,128)S(1)}, f32[3,3,2048]{2,1,0:T(4,128)}, u32[]{:S(2)}) copy-start(f32[3,3,2048]{2,1,0:T(4,128)} %param.9) | copy-start | bytes 221188
  0.0 19.8 %copy-start.3 = (bf16[256,3,2048]{2,0,1:T(8,128)(2,1)S(1)}, bf16[256,3,2048]{2,0,1:T(8,128)(2,1)}, u32[]{:S(2)}) copy-start(bf16[256,3,2048]{2,0,1:T(8,128)(2,1)} %param.8) | copy-start | bytes 9437188
  1.6 28.2 %collective-permute-start = (bf16[2,4096]{1,0:T(2,128)(2,1)}, bf16[2,4096]{1,0:T(2,128)(2,1)}, u32[]{:S(2)}, u32[]{:S(2)}) collective-permute-start(bf16[2,4096]{1,0:T(2,128)(2,1)} %slice.9), channel_id=1, source_target_pairs={{0,2},{2,4},{4,6},{6,8},{8,10},{10,12},{12,14},{14,16},{16,18},{18... | collective-permute-start | bytes 49160 | tf_op jit(solution)/shard_map/ppermute | solution.py:20
  24.7 2.8 copy-start.4
  356.3 7.8 %copy-start.2 = (bf16[2,512,2048]{2,1,0:T(8,128)(2,1)S(1)}, bf16[2,512,2048]{2,1,0:T(8,128)(2,1)}, u32[]{:S(2)}) copy-start(bf16[2,512,2048]{2,1,0:T(8,128)(2,1)} %spread.1) | copy-start | bytes 12582916
  364.1 9.2 %copy-start.1 = (f32[3,3,2048]{2,1,0:T(4,128)S(1)}, f32[3,3,2048]{2,1,0:T(4,128)}, u32[]{:S(2)}) copy-start(f32[3,3,2048]{2,1,0:T(4,128)} %param.9) | copy-start | bytes 221188
where the time goes:
time: 375 us; the launch traced here: 373 us
  Pallas kernels  291 us (78%)
  matrix products  53.2 us (14%)
  local copies, waits for them, and re-layouts  16.2 us (4%)
  other arithmetic  10.3 us (3%)
    pallas_call x1, Pallas kernels, gathered(): pl.pallas_call(gather_kernel, out_shape=[jax.ShapeDtypeStruct((4, HALO +...  189 us
    pallas_call x1, Pallas kernels, spread(): pl.pallas_call(spread_kernel, out_shape=jax.ShapeDtypeStruct((n_tp, count...  51.3 us
    dot_general x1, matrix products, shards(): jnp.dot(tok.reshape(-1, tok.shape[2]), weights.reshape(-1, weights.shape[...  34.5 us
    pallas_call x1, Pallas kernels, convolved(): pl.pallas_call(functools.partial(conv_kernel, width), grid=(steps, segmen...  25.3 us
    pallas_call x1, Pallas kernels, shared(): pl.pallas_call(share_kernel, out_shape=jax.ShapeDtypeStruct((total,) + st...  16 us
    pallas_call x1, Pallas kernels, mixed_of(): pl.pallas_call(functools.partial(mix_kernel, width), grid=(chans // lanes...  9.22 us
    dot_general x1, matrix products, shards(): jnp.dot(full[d], out_rows[d - 1], preferred_element_type=jnp.float32)  9.2 us
    dot_general x1, matrix products, shards(): total = jnp.dot(full[0], kept, preferred_element_type=jnp.float32)  7.73 us
  transfers between devices with their start and end apart: 1, of which 0 were waited for; matrix products, arithmetic and copies ran while one was open for 7% of the time, Pallas kernels for 0%

commit v1 on v0

--- a/solution.py
+++ b/solution.py
@@ -9,6 +9,7 @@
 
 SUB = 128
 LANES = 256
+BLOCK = 128
 HALO = 16
 MESH = pl.DeviceIdType.MESH
 HIGHEST = lax.Precision.HIGHEST
@@ -96,17 +97,17 @@
 
 def convolved(proj, taps, lags, leave, reach, fade, skip, width, order, count):
     chans = skip.shape[1]
-    lanes = min(LANES, chans)
+    lanes = min(BLOCK, chans)
     steps = chans // lanes
     tile = lanes // width
-    segments, rows, _ = proj.shape
+    _, segments, rows, _ = proj.shape
     return pl.pallas_call(
         functools.partial(conv_kernel, width),
         grid=(steps, segments),
         in_specs=[
-            pl.BlockSpec((None, rows, lanes), lambda i, j: (j, 0, i)),
-            pl.BlockSpec((None, rows, lanes), lambda i, j: (j, 0, steps + i)),
-            pl.BlockSpec((None, rows, lanes), lambda i, j: (j, 0, 2 * steps + i)),
+            pl.BlockSpec((None, None, rows, lanes), lambda i, j: (i, j, 0, 0)),
+            pl.BlockSpec((None, None, rows, lanes), lambda i, j: (i, j, 0, 1)),
+            pl.BlockSpec((None, None, rows, lanes), lambda i, j: (i, j, 0, 2)),
             pl.BlockSpec((taps.shape[0], 3, lanes), lambda i, j: (0, 0, i)),
             pl.BlockSpec((tile, SUB), lambda i, j: (i, 0)),
             pl.BlockSpec((tile * order, SUB), lambda i, j: (i, 0)),
@@ -160,7 +161,7 @@
 
 
 def gather_kernel(
-    own_ref, halo_ref, pieces_ref, out_ref, tok_ref, w_ref, wo_ref, held_ref, held_w_ref, local_sems,
+    own_ref, halo_ref, w3_ref, out_ref, proj_ref, wo_ref, tok_ref, w_ref, acc_ref, local_sems, own_sems,
     line_send, line_recv, pass_send, pass_recv, pair_send, pair_recv,
     tp_send, tp_recv, core_send, core_recv, early_send, early_recv,
     cols_send, cols_recv, swap_send, swap_recv, halo_send, halo_recv,
@@ -171,6 +172,9 @@
     mine = index_of(z, x, core)
     side = {"seq": index_of(z, 1 - x, core)}
     twin = {"seq": index_of(z, x, 1 - core)}
+    blocks, _, _, lanes = w_ref.shape
+    rows = w3_ref.shape[1]
+    total = blocks * depth
 
     def on_line(hop):
         there = z ^ hop[0]
@@ -192,16 +196,9 @@
     body = pl.ds(HALO, own_ref.shape[0])
     head = pl.ds(0, HALO)
     taken = [
-        pltpu.make_async_copy(own_ref, held_ref.at[body], local_sems.at[0]),
-        pltpu.make_async_copy(halo_ref, held_ref.at[head], local_sems.at[1]),
-        pltpu.make_async_copy(pieces_ref.at[own_slot], held_w_ref, local_sems.at[2]),
+        pltpu.make_async_copy(own_ref, tok_ref.at[own_slot, body], local_sems.at[0]),
+        pltpu.make_async_copy(halo_ref, tok_ref.at[own_slot, head], local_sems.at[1]),
     ]
-    stay = [
-        pltpu.make_async_copy(held_ref, tok_ref.at[own_slot], local_sems.at[3]),
-        pltpu.make_async_copy(held_w_ref, w_ref.at[mine], local_sems.at[4]),
-    ]
-    for copy in taken:
-        copy.start()
     started = []
 
     def begin(*what):
@@ -210,13 +207,49 @@
         started.append(copy)
         return copy
 
-    def to_line(hop):
+    def wide(role, block):
+        return w3_ref.at[:, :, pl.ds(pl.multiple_of((role * blocks + block) * lanes, lanes), lanes)]
+
+    def landed(block, source):
+        return w_ref.at[block, :, pl.ds(pl.multiple_of(source * rows, rows), rows), :]
+
+    def own_piece(block):
+        return pltpu.make_async_copy(wide(own_slot, block), landed(block, mine), own_sems.at[block])
+
+    def first(block):
+        return remote(
+            wide(own_slot, block), landed(block, mine),
+            pass_send.at[block, 0], pass_recv.at[block, 0], side,
+        )
+
+    def line(block, hop):
         there, which = on_line(hop)
         index = 2 * hop[0] + hop[1]
-        return begin(
-            pieces_ref.at[2 * lax.rem(there, 2) + which], w_ref.at[mine],
-            line_send.at[index], line_recv.at[index], {"seq": index_of(there, x, which)},
-        )
+        return remote(
+            wide(2 * lax.rem(there, 2) + which, block), landed(block, mine),
+            line_send.at[block, index], line_recv.at[block, index], {"seq": index_of(there, x, which)},
+        )
+
+    def arriving(block, hop):
+        there, which = on_line(hop)
+        index = 2 * hop[0] + hop[1]
+        where = landed(block, index_of(there, x, which))
+        return remote(
+            where, where, line_send.at[block, index], line_recv.at[block, index],
+            {"seq": index_of(there, x, which)},
+        )
+
+    def passing(block, hop):
+        there, which = on_line(hop)
+        index = 2 * hop[0] + hop[1]
+        where = landed(block, index_of(there, x, which))
+        return remote(where, where, pass_send.at[block, index], pass_recv.at[block, index], side)
+
+    def passed(block, hop):
+        there, which = on_line(hop)
+        index = 2 * hop[0] + hop[1]
+        where = landed(block, index_of(there, 1 - x, which))
+        return remote(where, where, pass_send.at[block, index], pass_recv.at[block, index], side)
 
     def to_pair(piece):
         where = tok_ref.at[own_slot, body, band(part, piece)]
@@ -245,16 +278,23 @@
         where = wo_ref.at[d - 1, quarter_rows(piece)]
         return begin(where, where, swap_send.at[slot], swap_recv.at[slot], twin)
 
+    for copy in taken:
+        copy.start()
+
+    def issue(block):
+        own_piece(block).start()
+        first(block).start()
+        for hop in hops:
+            line(block, hop).start()
+
     paired = [to_pair(0)]
-    first = begin(
-        pieces_ref.at[own_slot], w_ref.at[mine], pass_send.at[0], pass_recv.at[0], side
-    )
-    line = {}
-    for hop in hops[:2]:
-        line[hop] = to_line(hop)
+    own_piece(0).start()
+    first(0).start()
+    for hop in hops[:3]:
+        line(0, hop).start()
     paired.append(to_pair(1))
-    for hop in hops[2:]:
-        line[hop] = to_line(hop)
+    for hop in hops[3:]:
+        line(0, hop).start()
     moved = {(d, 0): columns(d, 0) for d in range(1, n_tp)}
     early = begin(own_ref, tok_ref.at[own_slot, body], early_send, early_recv, twin)
     heads = []
@@ -264,20 +304,17 @@
             halo_ref, tok_ref.at[own_slot, head], halo_send.at[n], halo_recv.at[n],
             {"seq": index_of(there, x, which)},
         ))
-    for copy in taken:
-        copy.wait()
-    for copy in stay:
-        copy.start()
-
-    forwards = []
-
-    def hand_on(hop):
-        index = 2 * hop[0] + hop[1]
-        source = index_of(on_line(hop)[0], x, on_line(hop)[1])
-        line[hop].wait_recv()
-        forwards.append(begin(
-            w_ref.at[source], w_ref.at[source], pass_send.at[index], pass_recv.at[index], side
-        ))
+
+    def forward(n):
+        block, step = n // depth, lax.rem(n, depth)
+
+        @pl.when(step > 0)
+        def _():
+            arriving(block, (step, 0)).wait_recv()
+            passing(block, (step, 0)).start()
+
+        arriving(block, (step, 1)).wait_recv()
+        passing(block, (step, 1)).start()
 
     twins, across = [], {}
 
@@ -296,54 +333,136 @@
             )
         to_twin(part, piece, 0)
 
-    hand_on(hops[0])
+    forward(0)
     pair_on(0)
-    hand_on(hops[1])
-    hand_on(hops[3])
+    forward(1)
     pair_on(1)
     for d in range(1, n_tp):
         moved[d, 1] = columns(d, 1)
-    hand_on(hops[2])
-    for hop in hops[4:]:
-        hand_on(hop)
+    if blocks > 1:
+        issue(1)
+    for n in range(2, depth):
+        forward(n)
+    for piece in range(2):
+        for d in range(1, n_tp):
+            across[d, piece].wait_recv()
+            to_twin(lax.rem(part - d + n_tp, n_tp), piece, d)
+    for copy in taken:
+        copy.wait()
+    for copy in [early] + heads + twins:
+        copy.wait_recv()
+
+    depth_rows = 4 * rows
+
+    def compute(n):
+        block, step = n // depth, lax.rem(n, depth)
+
+        @pl.when(step == 0)
+        def _():
+            own_piece(block).wait()
+
+        for other in range(2):
+            passed(block, (step, other)).wait_recv()
+        span = pl.ds(pl.multiple_of((z ^ step) * depth_rows, depth_rows), depth_rows)
+
+        def one(slot, carry):
+            right = jnp.concatenate([w_ref[block, p, span, :] for p in range(3)], axis=1)
+            value = jnp.dot(tok_ref[slot, :, span], right, preferred_element_type=jnp.float32)
+
+            @pl.when(step == 0)
+            def _():
+                acc_ref[slot] = value
+
+            @pl.when(step > 0)
+            def _():
+                acc_ref[slot] = acc_ref[slot] + value
+
+            return carry
+
+        lax.fori_loop(0, 4, one, 0)
+
+        @pl.when(step == depth - 1)
+        def _():
+            def put(slot, carry):
+                for p in range(3):
+                    proj_ref[block, slot, :, p * lanes : (p + 1) * lanes] = acc_ref[
+                        slot, :, p * lanes : (p + 1) * lanes
+                    ].astype(proj_ref.dtype)
+                return carry
+
+            lax.fori_loop(0, 4, put, 0)
+
+    lag = min(2, depth)
+
+    def early_step(n, carry):
+        compute(n)
+        return carry
+
+    lax.fori_loop(0, depth - lag, early_step, 0)
+
+    def step(n, carry):
+        block = n // depth
+
+        @pl.when((lax.rem(n, depth) == 0) & (block + 1 < blocks))
+        def _():
+            issue(block + 1)
+
+        forward(n)
+        compute(n - lag)
+        return carry
+
+    lax.fori_loop(depth, total, step, 0)
     for piece in range(2):
         for d in range(1, n_tp):
             moved[d, piece].wait_recv()
-            twins.append(swap(d, piece))
-            across[d, piece].wait_recv()
-            to_twin(lax.rem(part - d + n_tp, n_tp), piece, d)
-    for copy in [first, early] + heads + forwards + twins:
+            twins_swap = swap(d, piece)
+            heads.append(twins_swap)
+    lax.fori_loop(total - lag, total, early_step, 0)
+    for copy in heads[3:]:
         copy.wait_recv()
     for copy in started:
         copy.wait_send()
-    for copy in stay:
-        copy.wait()
-
-
-def gathered(own, halo, pieces, w_out):
+
+    def finish(block, carry):
+        first(block).wait_send()
+        for hop in hops:
+            line(block, hop).wait_send()
+            passing(block, hop).wait_send()
+        return carry
+
+    lax.fori_loop(0, blocks, finish, 0)
+
+
+def gathered(own, halo, w3, w_out):
     size, n_tp = lax.axis_size("seq"), lax.axis_size("tp")
     line = size // 2
+    chans = w3.shape[2] // 4
+    lanes = min(BLOCK, chans)
+    blocks = chans // lanes
+    tall = HALO + own.shape[0]
     anywhere = pl.BlockSpec(memory_space=pl.ANY)
-    counts = [5, line, line, line, line, 2, 2] + [2 * n_tp] * 4 + [0, 0] + [2 * n_tp] * 4 + [3, 3]
+    counts = [3, blocks] + [(blocks, line)] * 4 + [2, 2] + [2 * n_tp] * 4 + [0, 0] + [2 * n_tp] * 4 + [3, 3]
     return pl.pallas_call(
         gather_kernel,
         out_shape=[
-            jax.ShapeDtypeStruct((4, HALO + own.shape[0], own.shape[1]), own.dtype),
-            jax.ShapeDtypeStruct((size,) + pieces.shape[1:], pieces.dtype),
+            jax.ShapeDtypeStruct((blocks, 4, tall, 3 * lanes), own.dtype),
             jax.ShapeDtypeStruct(
                 (n_tp - 1, w_out.shape[0], w_out.shape[1] // n_tp), w_out.dtype
             ),
         ],
         in_specs=[anywhere] * 4,
-        out_specs=[anywhere] * 3,
+        out_specs=[pl.BlockSpec(memory_space=pltpu.VMEM), anywhere],
         scratch_shapes=[
-            pltpu.VMEM((HALO + own.shape[0], own.shape[1]), own.dtype),
-            pltpu.VMEM(pieces.shape[1:], pieces.dtype),
+            pltpu.VMEM((4, tall, own.shape[1]), own.dtype),
+            pltpu.VMEM((blocks, 3, own.shape[1], lanes), w3.dtype),
+            pltpu.VMEM((4, tall, 3 * lanes), jnp.float32),
         ]
-        + [pltpu.SemaphoreType.DMA((n,) if n else ()) for n in counts],
-        compiler_params=pltpu.CompilerParams(collective_id=0, has_side_effects=True),
+        + [pltpu.SemaphoreType.DMA(n if isinstance(n, tuple) else (n,) if n else ()) for n in counts],
+        compiler_params=pltpu.CompilerParams(
+            collective_id=0, has_side_effects=True, vmem_limit_bytes=60 << 20
+        ),
         name="gather",
-    )(own, halo, pieces, w_out)
+    )(own, halo, w3, w_out)
 
 
 def share_kernel(own_ref, all_ref, send_sems, recv_sems):
@@ -483,7 +602,7 @@
 
 def shards(tokens, w_in, short_taps, decay_rate, residue, skip_gain, w_out):
     count = tokens.shape[0]
-    rows, _, all_chans = w_in.shape
+    all_chans = w_in.shape[2]
     width = all_chans // decay_rate.shape[0]
     taps = short_taps.shape[0]
     z, x, core, depth = place()
@@ -494,8 +613,7 @@
 
     before = shifted_by(tokens[count - (taps - 1) :], "seq", 1)
     halo = jnp.pad(before, ((HALO - (taps - 1), 0), (0, 0)))
-    pieces = w_in.reshape(rows, 3, 4, chans).transpose(2, 0, 1, 3).reshape(4, rows, 3 * chans)
-    tok, weights, out_rows = gathered(tokens, halo, pieces, w_out)
+    proj, out_rows = gathered(tokens, halo, w_in.transpose(1, 0, 2), w_out)
 
     def own(array, axis):
         share = array.shape[axis] // 4
@@ -530,11 +648,6 @@
         ahead >= 0, jnp.exp(-by_mode * (count * jnp.maximum(ahead, 0).astype(jnp.float32))), 0.0
     )
 
-    proj = jnp.dot(
-        tok.reshape(-1, tok.shape[2]),
-        weights.reshape(-1, weights.shape[2]),
-        preferred_element_type=jnp.float32,
-    ).astype(jnp.bfloat16).reshape(4, -1, 3 * chans)
     query, base, final = convolved(
         proj, short_taps, lags, leave, reach, fade, skip, width, order, count
     )

time: 375 us -> 350 us (0.933)
  matrix products: 53.2 us -> 17.9 us
  Pallas kernels: 291 us -> 317 us
  local copies, waits for them, and re-layouts: 16.2 us -> 5.25 us
  other arithmetic: 10.3 us -> 4.78 us
    dot_general x1 -> x0, matrix products: 34.5 us -> none  [shards(): jnp.dot(tok.reshape(-1, tok.shape[2]), weights.reshape(-1, weights.shape[...]
    pallas_call x1, Pallas kernels: 189 us -> 219 us  [gathered(): pl.pallas_call(gather_kernel, out_shape=[jax.ShapeDtypeStruct((blocks, 4,...]
  transfers between devices with their start and end apart: 1 -> 1, of which waited for: 0 -> 0; matrix products, arithmetic and copies ran while one was open for 7% -> 3% of each run, Pallas kernels for 0% -> 0%
where the time goes in v1:
time: 350 us; the launch traced here: 348 us
  Pallas kernels  317 us (91%)
  matrix products  17.9 us (5%)
  local copies, waits for them, and re-layouts  5.25 us (2%)
  other arithmetic  4.78 us (1%)
    pallas_call x1, Pallas kernels, gathered(): pl.pallas_call(gather_kernel, out_shape=[jax.ShapeDtypeStruct((blocks, 4,...  219 us
    pallas_call x1, Pallas kernels, spread(): pl.pallas_call(spread_kernel, out_shape=jax.ShapeDtypeStruct((n_tp, count...  51.8 us
    pallas_call x1, Pallas kernels, convolved(): pl.pallas_call(functools.partial(conv_kernel, width), grid=(steps, segmen...  23.2 us
    pallas_call x1, Pallas kernels, shared(): pl.pallas_call(share_kernel, out_shape=jax.ShapeDtypeStruct((total,) + st...  13.9 us
    pallas_call x1, Pallas kernels, mixed_of(): pl.pallas_call(functools.partial(mix_kernel, width), grid=(chans // lanes...  9.27 us
    dot_general x1, matrix products, shards(): jnp.dot(full[d], out_rows[d - 1], preferred_element_type=jnp.float32)  9.17 us
    dot_general x1, matrix products, shards(): total = jnp.dot(full[0], kept, preferred_element_type=jnp.float32)  7.73 us
  transfers between devices with their start and end apart: 1, of which 0 were waited for; matrix products, arithmetic and copies ran while one was open for 3% of the time, Pallas kernels for 0%

profile of v1, /device:TPU:0, one launch (start us, length us, event | category | flops | bytes accessed | tf_op | source)
XLA Modules:
  0.0 347.7 jit_solution(8003494567014209005)
XLA Ops:
  0.0 0.0 copy-start
  0.0 0.9 slice.9
  0.9 2.4 collective-permute-start
  3.5 0.1 add_add_fusion
  3.5 0.1 add.186
  3.6 0.1 fusion.16
  3.7 0.1 subtract_compare_fusion
  3.8 0.8 multiply_exponential_fusion.1
  4.6 0.1 copy.12
  4.7 0.1 mul.153
  4.7 0.1 copy.10
  4.8 0.1 neg.48
  4.9 0.1 copy.15
  5.0 0.1 broadcast_in_dim.11
  5.1 0.2 neg.50
  5.3 0.8 multiply_exponential_fusion.leave_ref
  6.1 1.2 exponential_multiply_fusion.reach_ref
  7.3 1.0 fusion.10
  8.3 1.7 exponential_select_fusion.weight_ref
  10.0 0.6 constant_dynamic-slice_fusion.taps_ref
  10.6 0.1 copy.13
  10.7 0.9 exp.31.fade_ref
  11.6 1.3 dynamic-slice.3
  12.9 0.0 collective-permute-done
  12.9 0.7 pad.4.halo_ref
  13.6 219.0 %gather.1 = (bf16[4,4,528,384]{3,2,1,0:T(8,128)(2,1)}, bf16[1,2048,2048]{2,1,0:T(8,128)(2,1)}) custom-call(bf16[512,4096]{1,0:T(8,128)(2,1)} %own_ref.1, bf16[16,4096]{1,0:T(8,128)(2,1)} %pad.4.halo_ref, bf16[3,256,2048]{2,1,0:T(8,128)(2,1)} %bitcast.19, bf16[2048,4096]{1,0:T(8,128)(2,1)} %out_ref.1), custom_call_target="tpu_custom_call" | custom-call | tf_op jit(solution)/shard_map/gather/pallas_call | solution.py:445
  232.6 23.2 %conv.1 = (f32[4,512,512]{2,1,0:T(8,128)}, f32[4,512,512]{2,1,0:T(8,128)}, f32[4,16,512]{2,1,0:T(8,128)}) custom-call(bf16[4,4,528,384]{3,2,1,0:T(8,128)(2,1)} %get-tuple-element.10.q_ref.k_ref.v_ref, bf16[4,4,528,384]{3,2,1,0:T(8,128)(2,1)} %get-tuple-element.10.q_ref.k_ref.v_ref, bf16[4,4,528,384]{3,2,1,0:T(8,128)(2,1)} %get-tuple-element.10.q_ref.k_ref.v_ref, ...), custom_call_target="tpu_custom_call" | custom-call | flops 536870912 | bytes 5242880 | tf_op jit(solution)/shard_map/conv/pallas_call | solution.py:104
  255.8 13.9 %share.1 = f32[4,4,16,512]{3,2,1,0:T(8,128)} custom-call(f32[4,16,512]{2,1,0:T(8,128)} %get-tuple-element.13.own_ref), custom_call_target="tpu_custom_call" | custom-call | tf_op jit(solution)/shard_map/share/pallas_call | solution.py:493
  269.7 9.3 %mix.1.mix_ref = bf16[4,512,512]{2,1,0:T(8,128)(2,1)} custom-call(f32[4,512,512]{2,1,0:T(8,128)} %get-tuple-element.11.query_ref, f32[4,512,512]{2,1,0:T(8,128)} %get-tuple-element.12.base_ref, f32[16,16,512]{2,1,0:T(8,128)} %bitcast.20, f32[4,16,16,512]{3,2,1,0:T(8,128)} %exponential_select_fusion.weight_ref, f32[512,512]{1,0:T(8,128)} %exponential_multiply_fusion.reach_ref), custom_call_target="tpu_custom_call" | custom-call | tf_op jit(solution)/shard_map/mix/pallas_call | solution.py:587
  279.0 51.8 %spread.1 = bf16[2,512,2048]{2,1,0:T(8,128)(2,1)} custom-call(bf16[4,512,512]{2,1,0:T(8,128)(2,1)} %mix.1.mix_ref), custom_call_target="tpu_custom_call" | custom-call | tf_op jit(solution)/shard_map/spread/pallas_call | solution.py:558
  330.8 7.7 %fusion.2 = f32[512,2048]{1,0:T(8,128)S(1)} fusion(bf16[2048,4096]{1,0:T(8,128)(2,1)} %out_ref.1, s32[]{:T(128)S(6)} %select_n.100, bf16[2,512,2048]{2,1,0:T(8,128)(2,1)} %spread.1), kind=kOutput, calls=%fused_computation.2 | convolution fusion | flops 4294967296 | bytes 14680068 | tf_op jit(solution)/shard_map/dot_general | solution.py:659
  338.6 9.2 %add_convert_fusion = bf16[512,2048]{1,0:T(8,128)(2,1)} fusion(f32[512,2048]{1,0:T(8,128)S(1)} %fusion.2, bf16[1,2048,2048]{2,1,0:T(8,128)(2,1)} %get-tuple-element.14, bf16[2,512,2048]{2,1,0:T(8,128)(2,1)S(1)} %copy-done.1), kind=kOutput, calls=%fused_computation.4 | convolution fusion | flops 4297064448 | bytes 16777216 | tf_op jit(solution)/shard_map/dot_general | solution.py:661
  (9 shorter events, 0.1 us)
Async XLA Ops:
  0.0 10.0 %copy-start = (f32[3,3,2048]{2,1,0:T(4,128)S(1)}, f32[3,3,2048]{2,1,0:T(4,128)}, u32[]{:S(2)}) copy-start(f32[3,3,2048]{2,1,0:T(4,128)} %param.9) | copy-start | bytes 221188
  0.9 12.0 %collective-permute-start = (bf16[2,4096]{1,0:T(2,128)(2,1)S(1)}, bf16[2,4096]{1,0:T(2,128)(2,1)S(1)}, u32[]{:S(2)}, u32[]{:S(2)}) collective-permute-start(bf16[2,4096]{1,0:T(2,128)(2,1)S(1)} %slice.9), channel_id=1, source_target_pairs={{0,2},{2,4},{4,6},{6,8},{8,10},{10,12},{12,14},{14,16},{16,18},{18... | collective-permute-start | bytes 49160 | tf_op jit(solution)/shard_map/ppermute | solution.py:21
  330.8 7.8 %copy-start.1 = (bf16[2,512,2048]{2,1,0:T(8,128)(2,1)S(1)}, bf16[2,512,2048]{2,1,0:T(8,128)(2,1)}, u32[]{:S(2)}) copy-start(bf16[2,512,2048]{2,1,0:T(8,128)(2,1)} %spread.1) | copy-start | bytes 12582916

commit v2 on v1

v2 whole, which is shorter than its diff:
```python
import functools

import jax
import jax.numpy as jnp
from jax import lax
from jax.experimental import pallas as pl
from jax.experimental.pallas import tpu as pltpu
from jax.sharding import PartitionSpec as P

SUB = 128
BLOCK = 128
COLUMN_PIECES = 8
HALO = 16
MESH = pl.DeviceIdType.MESH
HIGHEST = lax.Precision.HIGHEST


def shifted_by(block, axis, distance):
    devices = range(lax.axis_size(axis))
    route = [(i - distance, i) for i in devices if i - distance in devices]
    return lax.ppermute(block, axis, route)


def fanned(state, width, order):
    lanes = state.shape[1]
    tile = lanes // width
    full = jnp.concatenate([state] * tile, axis=0)
    row = lax.broadcasted_iota(jnp.int32, full.shape, 0) // order
    lane = lax.broadcasted_iota(jnp.int32, full.shape, 1) // width
    return jnp.where(row == lane, full, 0.0)


def split(value):
    high = value.astype(jnp.bfloat16)
    return high, (value - high.astype(jnp.float32)).astype(jnp.bfloat16)


def product_split(a, b):
    (ah, al), (bh, bl) = a, b
    dot = functools.partial(jnp.dot, preferred_element_type=jnp.float32)
    return dot(ah, bh) + (dot(ah, bl) + dot(al, bh))


def place():
    size, here = lax.axis_size("seq"), lax.axis_index("seq")
    return here // 4, lax.rem(here // 2, 2), lax.rem(here, 2), size // 4


def index_of(z, x, core):
    return z * 4 + x * 2 + core


def greet(peers):
    barrier = pltpu.get_barrier_semaphore()
    for peer in peers:
        pl.semaphore_signal(barrier, inc=1, device_id=peer, device_id_type=MESH)
    pl.semaphore_wait(barrier, len(peers))


def remote(source, target, send_sem, recv_sem, peer):
    return pltpu.make_async_remote_copy(
        src_ref=source,
        dst_ref=target,
        send_sem=send_sem,
        recv_sem=recv_sem,
        device_id=peer,
        device_id_type=MESH,
    )


def hyena_kernel(
    width,
    own_ref, w3_ref, out_ref, taps_ref, lags_ref, leave_ref, reach_ref, fade_ref, skip_ref, mode_ref,
    mixed_ref, wo_ref,
    tok_ref, w_ref, acc_ref, proj_ref, toep_ref, query_ref, base_ref, all_ref, mix_ref, full_ref, total_ref,
    local_sems, own_sems,
    line_send, line_recv, pass_send, pass_recv, pair_send, pair_recv,
    tp_send, tp_recv, core_send, core_recv, early_send, early_recv,
    cols_send, cols_recv, swap_send, swap_recv, halo_send, halo_recv,
    share_send, share_recv, role_send, role_recv, over_send, over_recv,
):
    z, x, core, depth = place()
    parity = lax.rem(z, 2)
    n_tp, part = lax.axis_size("tp"), lax.axis_index("tp")
    size = lax.axis_size("seq")
    mine = index_of(z, x, core)
    side = {"seq": index_of(z, 1 - x, core)}
    twin = {"seq": index_of(z, x, 1 - core)}
    blocks, _, _, lanes = w_ref.shape
    rows = w3_ref.shape[1]
    count = own_ref.shape[0]
    taps = taps_ref.shape[0]
    order = all_ref.shape[3]
    tile = lanes // width
    modes = tile * order
    total = blocks * depth

    def on_line(hop):
        there = z ^ hop[0]
        return there, (1 - core if hop[1] else core)

    hops = [(step, other) for step in range(depth) for other in range(2)][1:]
    tps = [{"tp": lax.rem(part + d, n_tp)} for d in range(1, n_tp)]
    greet([{"seq": lax.rem(mine + d, size)} for d in range(1, size)] + tps)

    cols = own_ref.shape[1] // (2 * n_tp)

    def band(which, piece):
        return pl.ds(pl.multiple_of((2 * which + piece) * cols, cols), cols)

    own_slot, mate_slot = 2 * parity + core, 2 * (1 - parity) + core
    body = pl.ds(HALO, count)
    edge = pl.ds(HALO // 2, HALO // 2)
    taken = pltpu.make_async_copy(own_ref, tok_ref.at[own_slot, body], local_sems.at[0])
    started = []

    def begin(*what):
        copy = remote(*what)
        copy.start()
        started.append(copy)
        return copy

    def wide(role, block):
        return w3_ref.at[:, :, pl.ds(pl.multiple_of((role * blocks + block) * lanes, lanes), lanes)]

    def landed(block, source):
        return w_ref.at[block, :, pl.ds(pl.multiple_of(source * rows, rows), rows), :]

    def own_piece(block):
        return pltpu.make_async_copy(wide(own_slot, block), landed(block, mine), own_sems.at[block])

    def first(block):
        return remote(
            wide(own_slot, block), landed(block, mine),
            pass_send.at[block, 0], pass_recv.at[block, 0], side,
        )

    def line(block, hop):
        there, which = on_line(hop)
        index = 2 * hop[0] + hop[1]
        return remote(
            wide(2 * lax.rem(there, 2) + which, block), landed(block, mine),
            line_send.at[block, index], line_recv.at[block, index], {"seq": index_of(there, x, which)},
        )

    def arriving(block, hop):
        there, which = on_line(hop)
        index = 2 * hop[0] + hop[1]
        where = landed(block, index_of(there, x, which))
        return remote(
            where, where, line_send.at[block, index], line_recv.at[block, index],
            {"seq": index_of(there, x, which)},
        )

    def passing(block, hop):
        there, which = on_line(hop)
        index = 2 * hop[0] + hop[1]
        where = landed(block, index_of(there, x, which))
        return remote(where, where, pass_send.at[block, index], pass_recv.at[block, index], side)

    def passed(block, hop):
        there, which = on_line(hop)
        index = 2 * hop[0] + hop[1]
        where = landed(block, index_of(there, 1 - x, which))
        return remote(where, where, pass_send.at[block, index], pass_recv.at[block, index], side)

    def to_pair(piece):
        where = tok_ref.at[own_slot, body, band(part, piece)]
        return begin(
            own_ref.at[:, band(part, piece)], where, pair_send.at[piece], pair_recv.at[piece],
            {"seq": index_of(z ^ 1, x, core)},
        )

    portion = wo_ref.shape[1] // (2 * COLUMN_PIECES)
    out_cols = wo_ref.shape[2]

    def portion_rows(piece):
        return pl.ds(pl.multiple_of((COLUMN_PIECES * core + piece) * portion, portion), portion)

    def out_span(which):
        return pl.ds(pl.multiple_of(which * out_cols, out_cols), out_cols)

    moved = {}

    def columns(pieces):
        for piece in pieces:
            for d in range(1, n_tp):
                slot = COLUMN_PIECES * (d - 1) + piece
                moved[d, piece] = begin(
                    out_ref.at[portion_rows(piece), out_span(lax.rem(part + d, n_tp))],
                    wo_ref.at[d - 1, portion_rows(piece)],
                    cols_send.at[slot], cols_recv.at[slot], tps[d - 1],
                )

    def swap(d, piece):
        slot = COLUMN_PIECES * (d - 1) + piece
        where = wo_ref.at[d - 1, portion_rows(piece)]
        return begin(where, where, swap_send.at[slot], swap_recv.at[slot], twin)

    after = jnp.where(x == 0, z, z + 1)
    leads = (core == 1) & ((x == 0) | (z < depth - 1))

    def edges():
        copies = []
        for n in range(4):
            slot = 2 * lax.rem(after, 2)
            copies.append(remote(
                own_ref.at[pl.ds(count - HALO // 2, HALO // 2)], tok_ref.at[slot, edge],
                halo_send.at[n], halo_recv.at[lax.rem(after, 2)],
                {"seq": index_of(after ^ (n // 2), 1 - x, n % 2)},
            ))
        return copies

    inner = (lax.rem(z, 4) == 1) | (lax.rem(z, 4) == 2)

    def step_of(n):
        turn = lax.rem(n, depth)
        rolled = lax.rem(turn + depth - 3, depth - 1) + 1
        return jnp.where(inner & (turn > 0), rolled, turn)

    def forward(n):
        block, step = n // depth, step_of(n)
        for other in range(2):
            arriving(block, (step, other)).wait_recv()
            passing(block, (step, other)).start()

    def forward_ahead(block, carry):
        forward(block * depth + 1)
        return carry

    def near(block, carry):
        arriving(block, (0, 1)).wait_recv()
        passing(block, (0, 1)).start()
        return carry

    def begin_own(block, carry):
        own_piece(block).start()
        first(block).start()
        line(block, (0, 1)).start()
        return carry

    def issue_step(block, step):
        for other in range(2):
            line(block, (step, other)).start()

    def issue(block):
        @pl.when(jnp.logical_not(inner))
        def _():
            issue_step(block, depth - 1)

        for step in range(1, depth - 1):
            issue_step(block, step)

    def issue_ahead(block, carry):
        issue_step(block, depth - 1)
        return carry

    taken.start()
    columns(range(2))
    paired = [to_pair(0), to_pair(1)]
    lax.fori_loop(0, blocks, begin_own, 0)

    @pl.when(leads)
    def _():
        for copy in edges():
            copy.start()

    @pl.when(inner)
    def _():
        lax.fori_loop(0, blocks, issue_ahead, 0)

    issue(0)
    early = begin(own_ref, tok_ref.at[own_slot, body], early_send, early_recv, twin)
    twins, across = [], {}

    def to_twin(which, piece, d):
        where = tok_ref.at[mate_slot, body, band(which, piece)]
        slot = 2 * d + piece
        twins.append(begin(where, where, core_send.at[slot], core_recv.at[slot], twin))

    def pair_on(piece):
        paired[piece].wait_recv()
        where = tok_ref.at[mate_slot, body, band(part, piece)]
        for d in range(1, n_tp):
            slot = 2 * (d - 1) + piece
            across[d, piece] = begin(
                where, where, tp_send.at[slot], tp_recv.at[slot], tps[d - 1]
            )
        to_twin(part, piece, 0)

    lax.fori_loop(0, blocks, near, 0)
    if blocks > 1:
        issue(1)
    half = blocks // 2

    @pl.when(inner)
    def _():
        lax.fori_loop(0, half, forward_ahead, 0)

    pair_on(0)
    columns(range(2, 3))

    @pl.when(inner)
    def _():
        lax.fori_loop(half, blocks, forward_ahead, 0)

    pair_on(1)
    columns(range(3, COLUMN_PIECES))

    @pl.when(jnp.logical_not(inner))
    def _():
        forward(1)

    for n in range(2, depth):
        forward(n)
    for piece in range(2):
        for d in range(1, n_tp):
            across[d, piece].wait_recv()
            to_twin(lax.rem(part - d + n_tp, n_tp), piece, d)
    taken.wait()
    for copy in [early] + twins:
        copy.wait_recv()
    for p in range(2):
        starts = (z - parity + p == 0) & (x == 0)

        @pl.when(starts)
        def _():
            tok_ref[2 * p, HALO // 2 : HALO] = jnp.zeros(
                (HALO // 2, tok_ref.shape[2]), tok_ref.dtype
            )

        @pl.when(jnp.logical_not(starts))
        def _():
            where = tok_ref.at[2 * p, edge]
            remote(where, where, halo_send.at[0], halo_recv.at[p], side).wait_recv()

        tok_ref[2 * p + 1, HALO // 2 : HALO] = tok_ref[2 * p, HALO // 2 + count : HALO + count]

    depth_rows = 4 * rows

    def compute(n):
        block, step = n // depth, step_of(n)

        @pl.when(step == 0)
        def _():
            own_piece(block).wait()

        for other in range(2):
            passed(block, (step, other)).wait_recv()
        span = pl.ds(pl.multiple_of((z ^ step) * depth_rows, depth_rows), depth_rows)

        def one(slot, carry):
            right = jnp.concatenate([w_ref[block, p, span, :] for p in range(3)], axis=1)
            value = jnp.dot(tok_ref[slot, :, span], right, preferred_element_type=jnp.float32)

            @pl.when(step == 0)
            def _():
                acc_ref[slot] = value

            @pl.when(step != 0)
            def _():
                acc_ref[slot] = acc_ref[slot] + value

            return carry

        lax.fori_loop(0, 4, one, 0)

        @pl.when(lax.rem(n, depth) == depth - 1)
        def _():
            def put(slot, carry):
                proj_ref[slot] = acc_ref[slot].astype(proj_ref.dtype)
                return carry

            lax.fori_loop(0, 4, put, 0)

    team = (z // 2) * 2 + x
    lane = lax.broadcasted_iota(jnp.int32, (SUB, 2 * lanes), 1)
    lane = lax.rem(lane, lanes) // width
    diagonal = (
        lax.broadcasted_iota(jnp.int32, (modes, lanes), 0) // order
        == lax.broadcasted_iota(jnp.int32, (modes, lanes), 1) // width
    )

    def chan(block):
        return pl.ds(pl.multiple_of((own_slot * blocks + block) * lanes, lanes), lanes)

    def convolve(block):
        below = lax.broadcasted_iota(jnp.int32, (SUB, SUB), 0) >= lax.broadcasted_iota(
            jnp.int32, (SUB, SUB), 1
        )
        lags = lags_ref[pl.ds(pl.multiple_of(block * tile, tile), tile)]
        for g in range(tile):
            turned = pltpu.roll(
                jnp.broadcast_to(lags[g : g + 1], (SUB, SUB)), 0, 1, stride=1, stride_axis=0
            )
            toep_ref[g * SUB : (g + 1) * SUB] = jnp.where(below, turned, 0.0).astype(jnp.bfloat16)
        span = pl.ds(pl.multiple_of(block * modes, modes), modes)
        leave = split(leave_ref[span])
        reach = split(reach_ref[block, :SUB])
        fade = fade_ref[span]
        skip = skip_ref[:, chan(block)]
        skip = jnp.concatenate([skip, skip], axis=1)
        kernel_taps = [[taps_ref[tap, w : w + 1, chan(block)] for w in range(3)] for tap in range(taps)]

        def segment(slot, carry):
            def filtered(which):
                value = proj_ref[slot, :, which * lanes : (which + 1) * lanes].astype(jnp.float32)
                out = None
                for tap in range(taps):
                    term = kernel_taps[tap][which] * value[HALO - tap : HALO - tap + count]
                    out = term if out is None else out + term
                return out

            query_ref[slot] = filtered(0)
            gated = filtered(1) * filtered(2)
            state = jnp.zeros((modes, lanes), jnp.float32)
            for two in range(count // SUB // 2):
                low, high = 2 * two * SUB, (2 * two + 1) * SUB
                piece = jnp.concatenate([gated[low:high], gated[high : high + SUB]], axis=1)
                spread = jnp.dot(
                    toep_ref[...], piece.astype(jnp.bfloat16), preferred_element_type=jnp.float32
                )
                picked = spread[:SUB]
                for g in range(1, tile):
                    picked = jnp.where(lane == g, spread[g * SUB : (g + 1) * SUB], picked)
                local = skip * piece + picked
                fresh = product_split(leave, split(piece))
                for turn, start in ((0, low), (1, high)):
                    value = local[:, turn * lanes : (turn + 1) * lanes]
                    if start:
                        value = value + product_split(reach, split(state))
                    base_ref[slot, start : start + SUB] = value
                    state = fade * state + jnp.where(
                        diagonal, fresh[:, turn * lanes : (turn + 1) * lanes], 0.0
                    )
            compact = state[:order]
            for g in range(1, tile):
                compact = compact + state[g * order : (g + 1) * order]
            all_ref[block, team, slot] = compact
            return carry

        lax.fori_loop(0, 4, segment, 0)

    def teammate(d):
        there = lax.rem(team + d, depth)
        return there, {
            "seq": index_of(2 * (there // 2) + parity, lax.rem(there, 2), core)
        }

    def shares(block):
        return [
            remote(
                all_ref.at[block, team], all_ref.at[block, team],
                share_send.at[block, d - 1], share_recv.at[block, d - 1], teammate(d)[1],
            )
            for d in range(1, depth)
        ]

    def share_waits(block):
        return [
            remote(
                all_ref.at[block, lax.rem(team - d + depth, depth)],
                all_ref.at[block, lax.rem(team - d + depth, depth)],
                share_send.at[block, d - 1], share_recv.at[block, d - 1], teammate(d)[1],
            )
            for d in range(1, depth)
        ]

    def colleague(d):
        there, which = z ^ (d // 2), (1 - core if d % 2 else core)
        return 2 * lax.rem(there, 2) + which, {"seq": index_of(there, x, which)}

    def combine(block):
        for copy in share_waits(block):
            copy.wait_recv()
        rates = mode_ref[:, chan(block)]
        reach = split(reach_ref[block])

        def segment(slot, carry):
            here = index_of(z - parity + slot // 2, x, lax.rem(slot, 2))

            def member(n, entering):
                for other in range(4):
                    ahead = here - 1 - index_of(
                        2 * (n // 2) + other // 2, lax.rem(n, 2), other % 2
                    )
                    far = (count * jnp.maximum(ahead, 0)).astype(jnp.float32)
                    weight = jnp.where(ahead >= 0, jnp.exp(-rates * far), 0.0)
                    entering = entering + weight * all_ref[block, n, other]
                return entering

            entering = lax.fori_loop(0, depth, member, jnp.zeros((order, lanes), jnp.float32))
            carried = product_split(reach, split(fanned(entering, width, order)))
            mix_ref[block, slot] = (query_ref[slot] * (base_ref[slot] + carried)).astype(mix_ref.dtype)
            return carry

        lax.fori_loop(0, 4, segment, 0)
        full_ref[0, block, own_slot] = mix_ref[block, own_slot]

    def roles(block):
        return [
            remote(
                mix_ref.at[block, colleague(d)[0]], full_ref.at[0, block, own_slot],
                role_send.at[block, d - 1], role_recv.at[block, d - 1], colleague(d)[1],
            )
            for d in (2, 3, 1)
        ]

    def role_waits(block):
        return [
            remote(
                full_ref.at[0, block, colleague(d)[0]], full_ref.at[0, block, colleague(d)[0]],
                role_send.at[block, d - 1], role_recv.at[block, d - 1], colleague(d)[1],
            )
            for d in range(1, 4)
        ]

    def overs(block, n):
        which = colleague(n)[0]
        return [
            remote(
                full_ref.at[0, block, which], full_ref.at[d, block, which],
                over_send.at[block, 4 * (d - 1) + n], over_recv.at[block, 4 * (d - 1) + n], tps[d - 1],
            )
            for d in range(1, n_tp)
        ]

    def over_waits(block):
        return [
            remote(
                full_ref.at[d, block, colleague(n)[0]], full_ref.at[d, block, colleague(n)[0]],
                over_send.at[block, 4 * (d - 1) + n], over_recv.at[block, 4 * (d - 1) + n], tps[d - 1],
            )
            for n in range(4)
            for d in range(1, n_tp)
        ]

    def send_states(block):
        for copy in shares(block):
            copy.start()

    def send_mix(block):
        for copy in roles(block) + overs(block, 0):
            copy.start()

    def send_over(block):
        for n, copy in enumerate(role_waits(block)):
            copy.wait_recv()
            for across_copy in overs(block, n + 1):
                across_copy.start()

    lag = 2

    def late_step(n, carry):
        compute(n)
        return carry

    lax.fori_loop(0, depth - lag, late_step, 0)

    def step(n, carry):
        block, turn = n // depth, lax.rem(n, depth)

        @pl.when((turn == 0) & (block + 1 < blocks))
        def _():
            issue(block + 1)

        @pl.when((turn > 1) | ((turn == 1) & jnp.logical_not(inner)))
        def _():
            forward(n)

        compute(n - lag)

        @pl.when(turn == 1)
        def _():
            convolve(block - 1)
            send_states(block - 1)

        @pl.when(turn == 2)
        def _():
            combine(block - 1)
            send_mix(block - 1)

        @pl.when(turn == 3)
        def _():
            send_over(block - 1)

        return carry

    lax.fori_loop(depth, total, step, 0)
    lax.fori_loop(total - lag, total, late_step, 0)
    loads = []

    def load(source, slot, d):
        chans = blocks * lanes
        copy = pltpu.make_async_copy(
            source, tok_ref.at[slot, pl.ds(0, chans), pl.ds(d * out_cols, out_cols)],
            local_sems.at[1 + 4 * d + slot],
        )
        copy.start()
        loads.append(copy)

    def role_rows(slot):
        return pl.ds(slot * blocks * lanes, blocks * lanes)

    inside = twins + list(across.values())
    for copy in inside:
        copy.wait_send()
    for slot in range(4):
        load(out_ref.at[role_rows(slot), out_span(part)], slot, 0)
    convolve(blocks - 1)
    send_states(blocks - 1)
    combine(blocks - 1)
    send_mix(blocks - 1)
    swaps = []
    for piece in range(COLUMN_PIECES):
        for d in range(1, n_tp):
            moved[d, piece].wait_recv()
            swaps.append(swap(d, piece))
    send_over(blocks - 1)
    for copy in swaps:
        copy.wait_recv()
    for d in range(1, n_tp):
        for slot in range(4):
            load(wo_ref.at[d - 1, role_rows(slot)], slot, d)
    for copy in loads:
        copy.wait()
    strip = min(4 * SUB, out_cols)

    def project(block, carry):
        for copy in over_waits(block):
            copy.wait_recv()
        pairs = [(d, slot) for d in range(n_tp) for slot in range(4)]
        left = jnp.concatenate([full_ref[d, block, slot] for d, slot in pairs], axis=1)
        span = pl.ds(pl.multiple_of(block * lanes, lanes), lanes)

        def one(n, carry):
            right = jnp.concatenate(
                [
                    tok_ref[slot, span, pl.ds(pl.multiple_of(d * out_cols + n * strip, strip), strip)]
                    for d, slot in pairs
                ],
                axis=0,
            )
            value = jnp.dot(left, right, preferred_element_type=jnp.float32)
            where = pl.ds(pl.multiple_of(n * strip, strip), strip)

            @pl.when(block > 0)
            def _():
                total_ref[:, where] = total_ref[:, where] + value

            @pl.when(block == 0)
            def _():
                total_ref[:, where] = value

            return carry

        lax.fori_loop(0, out_cols // strip, one, 0)
        return carry

    lax.fori_loop(0, blocks, project, 0)
    mixed_ref[...] = total_ref[...].astype(mixed_ref.dtype)
    for copy in started:
        if all(copy is not other for other in inside):
            copy.wait_send()

    @pl.when(leads)
    def _():
        for copy in edges():
            copy.wait_send()

    def finish(block, carry):
        first(block).wait_send()
        for hop in hops:
            line(block, hop).wait_send()
            passing(block, hop).wait_send()
        for copy in shares(block) + roles(block):
            copy.wait_send()
        for n in range(4):
            for copy in overs(block, n):
                copy.wait_send()
        return carry

    lax.fori_loop(0, blocks, finish, 0)


def hyena(own, w3, w_out, taps, lags, leave, reach, fade, skip, by_mode, width):
    size, n_tp = lax.axis_size("seq"), lax.axis_size("tp")
    line, depth = size // 2, size // 4
    count = own.shape[0]
    chans = w3.shape[2] // 4
    lanes = min(BLOCK, chans)
    blocks = chans // lanes
    order = by_mode.shape[0]
    tall = HALO + count
    out_cols = w_out.shape[1] // n_tp
    anywhere = pl.BlockSpec(memory_space=pl.ANY)
    near = pl.BlockSpec(memory_space=pltpu.VMEM)
    counts = (
        [1 + 4 * n_tp, blocks] + [(blocks, line)] * 4 + [2, 2] + [2 * n_tp] * 4 + [0, 0]
        + [COLUMN_PIECES * n_tp] * 4 + [4, 2]
        + [(blocks, depth - 1)] * 2 + [(blocks, 3)] * 2 + [(blocks, 4 * n_tp)] * 2
    )
    return pl.pallas_call(
        functools.partial(hyena_kernel, width),
        out_shape=[
            jax.ShapeDtypeStruct((count, out_cols), jnp.bfloat16),
            jax.ShapeDtypeStruct((n_tp - 1, w_out.shape[0], out_cols), w_out.dtype),
        ],
        in_specs=[anywhere] * 3 + [near] * 7,
        out_specs=[near, anywhere],
        scratch_shapes=[
            pltpu.VMEM((4, tall, own.shape[1]), own.dtype),
            pltpu.VMEM((blocks, 3, own.shape[1], lanes), w3.dtype),
            pltpu.VMEM((4, tall, 3 * lanes), jnp.float32),
            pltpu.VMEM((4, tall, 3 * lanes), jnp.bfloat16),
            pltpu.VMEM((lanes // width * SUB, SUB), jnp.bfloat16),
            pltpu.VMEM((4, count, lanes), jnp.float32),
            pltpu.VMEM((4, count, lanes), jnp.float32),
            pltpu.VMEM((blocks, depth, 4, order, lanes), jnp.float32),
            pltpu.VMEM((blocks, 4, count, lanes), jnp.bfloat16),
            pltpu.VMEM((n_tp, blocks, 4, count, lanes), jnp.bfloat16),
            pltpu.VMEM((count, out_cols), jnp.float32),
        ]
        + [pltpu.SemaphoreType.DMA(n if isinstance(n, tuple) else (n,) if n else ()) for n in counts],
        compiler_params=pltpu.CompilerParams(
            collective_id=0, has_side_effects=True, vmem_limit_bytes=60 << 20
        ),
        name="hyena",
    )(own, w3, w_out, taps, lags, leave, reach, fade, skip, by_mode)[0]


def shards(tokens, w_in, short_taps, decay_rate, residue, skip_gain, w_out):
    count = tokens.shape[0]
    all_chans = w_in.shape[2]
    width = all_chans // decay_rate.shape[0]
    z, x, core, depth = place()
    role = 2 * lax.rem(z, 2) + core
    by_mode = jnp.repeat(decay_rate.T, width, axis=1)

    def own(array, axis):
        share = array.shape[axis] // 4
        return lax.dynamic_slice_in_dim(array, role * share, share, axis)

    decay_rate, residue = own(decay_rate, 0), own(residue, 0)
    groups, order = decay_rate.shape
    lanes = min(BLOCK, all_chans // 4)
    modes = lanes // width * order
    weight_mode = residue * jnp.sqrt(2.0 * decay_rate / order)
    offsets = jnp.arange(SUB, dtype=jnp.float32)
    back = (-jnp.arange(SUB) % SUB).astype(jnp.float32)
    lags = jnp.einsum(
        "gm,gmd->gd",
        weight_mode,
        jnp.exp(-decay_rate[:, :, None] * back[None, None, :]),
        precision=HIGHEST,
    )
    rate = decay_rate.reshape(groups * order)
    leave = jnp.exp(-rate[:, None] * (SUB - 1.0 - offsets[None, :]))
    fade = jnp.exp(-rate * SUB)[:, None]
    positions = jnp.arange(count, dtype=jnp.float32)
    rate = rate.reshape(-1, 1, modes)
    reach = weight_mode.reshape(-1, 1, modes) * jnp.exp(-rate * (positions[None, :, None] + 1.0))
    return hyena(
        tokens, w_in.transpose(1, 0, 2), w_out, short_taps, lags, leave, reach, fade,
        skip_gain[None], by_mode, width,
    )


def solution(mesh):
    in_specs = (
        P("seq", None),
        P("seq", None, "tp"),
        P(None, None, "tp"),
        P("tp", None),
        P("tp", None),
        P("tp"),
        P("tp", None),
    )
    out_specs = P("seq", "tp")
    return jax.shard_map(shards, mesh=mesh, in_specs=in_specs, out_specs=out_specs, check_vma=False)
```

time: 350 us -> 296 us (0.85)
  Pallas kernels: 317 us -> 285 us
  matrix products: 17.9 us -> 1.04 us
    pallas_call x5 -> x1, Pallas kernels: 317 us -> 285 us  [hyena(): pl.pallas_call(functools.partial(hyena_kernel, width), out_shape=[jax.Sha...]
    dot_general x2 -> x0, matrix products: 16.9 us -> none  [the longest x1 9.17 us: shards(): jnp.dot(full[d], out_rows[d - 1], preferred_element_type=jnp.float32)]
  transfers between devices with their start and end apart: 1 -> 0, of which waited for: 0 -> 0; matrix products, arithmetic and copies ran while one was open for 3% -> 0% of each run, Pallas kernels for 0% -> 0%
where the time goes in v2:
time: 296 us
  Pallas kernels  285 us (96%)
  local copies, waits for them, and re-layouts  6.9 us (2%)
    pallas_call x1, Pallas kernels, hyena(): pl.pallas_call(functools.partial(hyena_kernel, width), out_shape=[jax.Sha...  285 us

profile of v2, /device:TPU:0, one launch (start us, length us, event | category | flops | bytes accessed | tf_op | source)
XLA Modules:
  0.0 295.7 jit_solution(11399982868985077221)
XLA Ops:
  0.0 0.8 multiply_exponential_fusion.1
  0.8 0.1 copy.14
  0.9 0.1 copy.10
  1.0 0.1 neg.40
  1.1 0.1 neg.39
  1.1 0.1 copy.16
  1.2 1.0 fusion
  2.3 0.1 copy.12
  2.3 0.1 mul.84
  2.4 0.9 exp.27.fade_ref
  3.3 0.9 multiply_exponential_fusion.leave_ref
  4.2 1.2 exponential_multiply_fusion.reach_ref
  5.4 1.0 broadcast_in_dim.5
  6.4 1.3 reshape.68.mode_ref
  7.7 284.8 %hyena.1 = (bf16[512,2048]{1,0:T(8,128)(2,1)}, bf16[1,2048,2048]{2,1,0:T(8,128)(2,1)}) custom-call(bf16[512,4096]{1,0:T(8,128)(2,1)} %own_ref.1, bf16[3,256,2048]{2,1,0:T(8,128)(2,1)} %bitcast.7, bf16[2048,4096]{1,0:T(8,128)(2,1)} %out_ref.1, f32[3,3,2048]{2,1,0:T(4,128)} %taps_ref.1, f32[32,128]{1,0:T(8,128)} %bitcast.10, ...), custom_call_target="tpu_custom_call" | custom-call | tf_op jit(solution)/shard_map/hyena/pallas_call | solution.py:703
  292.5 3.2 %copy.19 = bf16[512,2048]{1,0:T(8,128)(2,1)} copy(bf16[512,2048]{1,0:T(8,128)(2,1)} %get-tuple-element.6) | data formatting | bytes 4194304
  (3 shorter events, 0.0 us)

commit v3 on v2

--- a/solution.py
+++ b/solution.py
@@ -93,7 +93,6 @@
     order = all_ref.shape[3]
     tile = lanes // width
     modes = tile * order
-    total = blocks * depth
 
     def on_line(hop):
         there = z ^ hop[0]
@@ -213,20 +212,25 @@
 
     inner = (lax.rem(z, 4) == 1) | (lax.rem(z, 4) == 2)
 
-    def step_of(n):
-        turn = lax.rem(n, depth)
+    def step_of(turn):
         rolled = lax.rem(turn + depth - 3, depth - 1) + 1
         return jnp.where(inner & (turn > 0), rolled, turn)
 
-    def forward(n):
-        block, step = n // depth, step_of(n)
+    def forward(block, step):
         for other in range(2):
             arriving(block, (step, other)).wait_recv()
             passing(block, (step, other)).start()
 
-    def forward_ahead(block, carry):
-        forward(block * depth + 1)
+    def forward_far(block, carry):
+        forward(block, depth - 1)
         return carry
+
+    def forward_slot(block, turn):
+        outer = 2 - turn if turn < 2 else turn + 1
+
+        @pl.when(jnp.logical_not(inner) | (turn < depth - 2))
+        def _():
+            forward(block, jnp.where(inner, turn + 1, outer))
 
     def near(block, carry):
         arriving(block, (0, 1)).wait_recv()
@@ -243,21 +247,20 @@
         for other in range(2):
             line(block, (step, other)).start()
 
-    def issue(block):
+    def issue(block, begin_step=1):
+        for step in range(begin_step, depth - 1):
+            issue_step(block, step)
+
         @pl.when(jnp.logical_not(inner))
         def _():
             issue_step(block, depth - 1)
 
-        for step in range(1, depth - 1):
-            issue_step(block, step)
-
-    def issue_ahead(block, carry):
+    def issue_far(block, carry):
         issue_step(block, depth - 1)
         return carry
 
-    taken.start()
+    paired = [to_pair(0), to_pair(1)]
     columns(range(2))
-    paired = [to_pair(0), to_pair(1)]
     lax.fori_loop(0, blocks, begin_own, 0)
 
     @pl.when(leads)
@@ -267,10 +270,15 @@
 
     @pl.when(inner)
     def _():
-        lax.fori_loop(0, blocks, issue_ahead, 0)
-
-    issue(0)
+        lax.fori_loop(0, blocks, issue_far, 0)
+        issue_step(0, 1)
+
+    @pl.when(jnp.logical_not(inner))
+    def _():
+        issue(0)
+
     early = begin(own_ref, tok_ref.at[own_slot, body], early_send, early_recv, twin)
+    taken.start()
     twins, across = [], {}
 
     def to_twin(which, piece, d):
@@ -289,34 +297,39 @@
         to_twin(part, piece, 0)
 
     lax.fori_loop(0, blocks, near, 0)
+    half = blocks // 2
+
+    @pl.when(inner)
+    def _():
+        lax.fori_loop(0, half, forward_far, 0)
+
+    pair_on(0)
+    columns(range(2, 4))
+
+    @pl.when(inner)
+    def _():
+        lax.fori_loop(half, blocks, forward_far, 0)
+
+    pair_on(1)
+    columns(range(4, COLUMN_PIECES))
+
+    @pl.when(inner)
+    def _():
+        for n in range(2, depth - 1):
+            issue_step(0, n)
+
     if blocks > 1:
         issue(1)
-    half = blocks // 2
-
-    @pl.when(inner)
-    def _():
-        lax.fori_loop(0, half, forward_ahead, 0)
-
-    pair_on(0)
-    columns(range(2, 3))
-
-    @pl.when(inner)
-    def _():
-        lax.fori_loop(half, blocks, forward_ahead, 0)
-
-    pair_on(1)
-    columns(range(3, COLUMN_PIECES))
-
-    @pl.when(jnp.logical_not(inner))
-    def _():
-        forward(1)
-
-    for n in range(2, depth):
-        forward(n)
-    for piece in range(2):
+
+    def tokens_on(piece):
         for d in range(1, n_tp):
             across[d, piece].wait_recv()
             to_twin(lax.rem(part - d + n_tp, n_tp), piece, d)
+
+    tokens_on(0)
+    forward_slot(0, 0)
+    forward_slot(0, 1)
+    tokens_on(1)
     taken.wait()
     for copy in [early] + twins:
         copy.wait_recv()
@@ -338,8 +351,8 @@
 
     depth_rows = 4 * rows
 
-    def compute(n):
-        block, step = n // depth, step_of(n)
+    def compute(block, turn):
+        step = step_of(turn)
 
         @pl.when(step == 0)
         def _():
@@ -365,7 +378,7 @@
 
         lax.fori_loop(0, 4, one, 0)
 
-        @pl.when(lax.rem(n, depth) == depth - 1)
+        @pl.when(turn == depth - 1)
         def _():
             def put(slot, carry):
                 proj_ref[slot] = acc_ref[slot].astype(proj_ref.dtype)
@@ -384,7 +397,7 @@
     def chan(block):
         return pl.ds(pl.multiple_of((own_slot * blocks + block) * lanes, lanes), lanes)
 
-    def convolve(block):
+    def prepare(block):
         below = lax.broadcasted_iota(jnp.int32, (SUB, SUB), 0) >= lax.broadcasted_iota(
             jnp.int32, (SUB, SUB), 1
         )
@@ -394,6 +407,8 @@
                 jnp.broadcast_to(lags[g : g + 1], (SUB, SUB)), 0, 1, stride=1, stride_axis=0
             )
             toep_ref[g * SUB : (g + 1) * SUB] = jnp.where(below, turned, 0.0).astype(jnp.bfloat16)
+
+    def convolve(block, begin_slot, end_slot):
         span = pl.ds(pl.multiple_of(block * modes, modes), modes)
         leave = split(leave_ref[span])
         reach = split(reach_ref[block, :SUB])
@@ -439,7 +454,7 @@
             all_ref[block, team, slot] = compact
             return carry
 
-        lax.fori_loop(0, 4, segment, 0)
+        lax.fori_loop(begin_slot, end_slot, segment, 0)
 
     def teammate(d):
         there = lax.rem(team + d, depth)
@@ -549,45 +564,49 @@
             for across_copy in overs(block, n + 1):
                 across_copy.start()
 
-    lag = 2
-
-    def late_step(n, carry):
-        compute(n)
-        return carry
-
-    lax.fori_loop(0, depth - lag, late_step, 0)
-
-    def step(n, carry):
-        block, turn = n // depth, lax.rem(n, depth)
-
-        @pl.when((turn == 0) & (block + 1 < blocks))
-        def _():
-            issue(block + 1)
-
-        @pl.when((turn > 1) | ((turn == 1) & jnp.logical_not(inner)))
-        def _():
-            forward(n)
-
-        compute(n - lag)
-
-        @pl.when(turn == 1)
-        def _():
-            convolve(block - 1)
+    def stage(block, carry):
+        @pl.when(block > 0)
+        def _():
+            forward_slot(block, 0)
+            compute(block - 1, depth - 1)
+            prepare(block - 1)
+            convolve(block - 1, 0, 4)
             send_states(block - 1)
 
-        @pl.when(turn == 2)
+            @pl.when(block + 1 < blocks)
+            def _():
+                issue(block + 1)
+
+            forward_slot(block, 1)
+
+        compute(block, 0)
+        for turn in range(2, depth - 1):
+            forward_slot(block, turn)
+        compute(block, 1)
+
+        @pl.when(block > 0)
         def _():
             combine(block - 1)
             send_mix(block - 1)
 
-        @pl.when(turn == 3)
-        def _():
-            send_over(block - 1)
+        for turn in range(2, depth - 1):
+            compute(block, turn)
+
+        @pl.when(block > 1)
+        def _():
+            send_over(block - 2)
 
         return carry
 
-    lax.fori_loop(depth, total, step, 0)
-    lax.fori_loop(total - lag, total, late_step, 0)
+    lax.fori_loop(0, blocks, stage, 0)
+    swaps = []
+    for piece in range(COLUMN_PIECES):
+        for d in range(1, n_tp):
+            moved[d, piece].wait_recv()
+            swaps.append(swap(d, piece))
+    compute(blocks - 1, depth - 1)
+    if blocks > 1:
+        send_over(blocks - 2)
     loads = []
 
     def load(source, slot, d):
@@ -607,16 +626,9 @@
         copy.wait_send()
     for slot in range(4):
         load(out_ref.at[role_rows(slot), out_span(part)], slot, 0)
-    convolve(blocks - 1)
+    prepare(blocks - 1)
+    convolve(blocks - 1, 0, 4)
     send_states(blocks - 1)
-    combine(blocks - 1)
-    send_mix(blocks - 1)
-    swaps = []
-    for piece in range(COLUMN_PIECES):
-        for d in range(1, n_tp):
-            moved[d, piece].wait_recv()
-            swaps.append(swap(d, piece))
-    send_over(blocks - 1)
     for copy in swaps:
         copy.wait_recv()
     for d in range(1, n_tp):
@@ -657,7 +669,11 @@
         lax.fori_loop(0, out_cols // strip, one, 0)
         return carry
 
-    lax.fori_loop(0, blocks, project, 0)
+    lax.fori_loop(0, half, project, 0)
+    combine(blocks - 1)
+    send_mix(blocks - 1)
+    send_over(blocks - 1)
+    lax.fori_loop(half, blocks, project, 0)
     mixed_ref[...] = total_ref[...].astype(mixed_ref.dtype)
     for copy in started:
         if all(copy is not other for other in inside):

time: 296 us -> 250 us (0.84)
  Pallas kernels: 285 us -> 239 us
    pallas_call x1, Pallas kernels: 285 us -> 239 us  [hyena(): pl.pallas_call(functools.partial(hyena_kernel, width), out_shape=[jax.Sha...]
where the time goes in v3:
time: 250 us; the launch traced here: 249 us
  Pallas kernels  239 us (96%)
  local copies, waits for them, and re-layouts  6.9 us (3%)
  other arithmetic  2.88 us (1%)
    pallas_call x1, Pallas kernels, hyena(): pl.pallas_call(functools.partial(hyena_kernel, width), out_shape=[jax.Sha...  239 us

profile of v3, /device:TPU:0, one launch (start us, length us, event | category | flops | bytes accessed | tf_op | source)
XLA Modules:
  0.0 249.4 jit_solution(2954768798873314633)
XLA Ops:
  0.0 0.8 multiply_exponential_fusion.1
  0.8 0.1 copy.14
  0.9 0.1 copy.10
  1.0 0.1 neg.40
  1.1 0.1 neg.39
  1.1 0.1 copy.16
  1.2 1.0 fusion
  2.3 0.1 copy.12
  2.3 0.1 mul.84
  2.4 0.9 exp.27.fade_ref
  3.3 0.9 multiply_exponential_fusion.leave_ref
  4.2 1.2 exponential_multiply_fusion.reach_ref
  5.4 1.0 broadcast_in_dim.5
  6.4 1.3 reshape.68.mode_ref
  7.7 238.5 %hyena.1 = (bf16[512,2048]{1,0:T(8,128)(2,1)}, bf16[1,2048,2048]{2,1,0:T(8,128)(2,1)}) custom-call(bf16[512,4096]{1,0:T(8,128)(2,1)} %own_ref.1, bf16[3,256,2048]{2,1,0:T(8,128)(2,1)} %bitcast.7, bf16[2048,4096]{1,0:T(8,128)(2,1)} %out_ref.1, f32[3,3,2048]{2,1,0:T(4,128)} %taps_ref.1, f32[32,128]{1,0:T(8,128)} %bitcast.10, ...), custom_call_target="tpu_custom_call" | custom-call | tf_op jit(solution)/shard_map/hyena/pallas_call | solution.py:719
  246.2 3.2 %copy.19 = bf16[512,2048]{1,0:T(8,128)(2,1)} copy(bf16[512,2048]{1,0:T(8,128)(2,1)} %get-tuple-element.6) | data formatting | bytes 4194304
  (3 shorter events, 0.0 us)

commit v4 on v3

--- a/solution.py
+++ b/solution.py
@@ -12,13 +12,6 @@
 COLUMN_PIECES = 8
 HALO = 16
 MESH = pl.DeviceIdType.MESH
-HIGHEST = lax.Precision.HIGHEST
-
-
-def shifted_by(block, axis, distance):
-    devices = range(lax.axis_size(axis))
-    route = [(i - distance, i) for i in devices if i - distance in devices]
-    return lax.ppermute(block, axis, route)
 
 
 def fanned(state, width, order):
@@ -68,11 +61,58 @@
     )
 
 
+def coefficients(
+    width, role, decay_ref, residue_ref, lags_ref, leave_ref, reach_ref, fade_ref, mode_ref
+):
+    order = decay_ref.shape[0]
+    groups = decay_ref.shape[1] // 4
+    blocks, _, lanes = mode_ref.shape
+    count, modes = reach_ref.shape[1:]
+
+    def own(ref):
+        whole = ref[...]
+        part = whole[:, :groups]
+        for n in range(1, 4):
+            part = jnp.where(role == n, whole[:, n * groups : (n + 1) * groups], part)
+        return part
+
+    rate = own(decay_ref)
+    gain = own(residue_ref) * jnp.sqrt(2.0 * rate / order)
+    place_in = lax.broadcasted_iota(jnp.int32, (order, SUB), 1)
+    back = jnp.where(place_in == 0, 0, SUB - place_in).astype(jnp.float32)
+    left = (SUB - 1 - place_in).astype(jnp.float32)
+    rows = lax.broadcasted_iota(jnp.int32, (order, modes), 0)
+    lane = lax.broadcasted_iota(jnp.int32, (order, modes), 1)
+    wide = lax.broadcasted_iota(jnp.int32, (order, lanes), 1) // width
+    later = lax.broadcasted_iota(jnp.int32, (count, modes), 0).astype(jnp.float32) + 1.0
+    per = lanes // width
+    for block in range(blocks):
+        by_rate = jnp.zeros((order, modes), jnp.float32)
+        by_gain = jnp.zeros((order, modes), jnp.float32)
+        by_lane = jnp.zeros((order, lanes), jnp.float32)
+        for n in range(per):
+            g = block * per + n
+            column = rate[:, g : g + 1]
+            strength = gain[:, g : g + 1]
+            span = slice(g * order, (g + 1) * order)
+            lags_ref[g : g + 1] = jnp.sum(strength * jnp.exp(-column * back), axis=0, keepdims=True)
+            leave_ref[span] = jnp.exp(-column * left)
+            fade_ref[span] = jnp.exp(-jnp.broadcast_to(column, (order, lanes)) * SUB)
+            by_rate = jnp.where(lane // order == n, column, by_rate)
+            by_gain = jnp.where(lane // order == n, strength, by_gain)
+            by_lane = jnp.where(wide == n, column, by_lane)
+        mode_ref[block] = by_lane
+        pick = rows == lax.rem(lane, order)
+        flat = jnp.sum(jnp.where(pick, by_rate, 0.0), axis=0, keepdims=True)
+        weight = jnp.sum(jnp.where(pick, by_gain, 0.0), axis=0, keepdims=True)
+        reach_ref[block] = weight * jnp.exp(-flat * later)
+
+
 def hyena_kernel(
     width,
-    own_ref, w3_ref, out_ref, taps_ref, lags_ref, leave_ref, reach_ref, fade_ref, skip_ref, mode_ref,
+    own_ref, w3_ref, out_ref, taps_ref, decay_ref, residue_ref, skip_ref,
     mixed_ref, wo_ref,
-    tok_ref, w_ref, acc_ref, proj_ref, toep_ref, query_ref, base_ref, all_ref, mix_ref, full_ref, total_ref,
+    lags_ref, leave_ref, reach_ref, fade_ref, mode_ref, tok_ref, w_ref, acc_ref, proj_ref, toep_ref, query_ref, base_ref, all_ref, mix_ref, full_ref, total_ref,
     local_sems, own_sems,
     line_send, line_recv, pass_send, pass_recv, pair_send, pair_recv,
     tp_send, tp_recv, core_send, core_recv, early_send, early_recv,
@@ -213,8 +253,11 @@
     inner = (lax.rem(z, 4) == 1) | (lax.rem(z, 4) == 2)
 
     def step_of(turn):
-        rolled = lax.rem(turn + depth - 3, depth - 1) + 1
-        return jnp.where(inner & (turn > 0), rolled, turn)
+        if turn == 0:
+            return 0
+        return jnp.where(
+            inner, (turn + depth - 3) % (depth - 1) + 1, 3 - turn if turn < 3 else turn
+        )
 
     def forward(block, step):
         for other in range(2):
@@ -297,6 +340,9 @@
         to_twin(part, piece, 0)
 
     lax.fori_loop(0, blocks, near, 0)
+    coefficients(
+        width, own_slot, decay_ref, residue_ref, lags_ref, leave_ref, reach_ref, fade_ref, mode_ref
+    )
     half = blocks // 2
 
     @pl.when(inner)
@@ -304,14 +350,13 @@
         lax.fori_loop(0, half, forward_far, 0)
 
     pair_on(0)
-    columns(range(2, 4))
 
     @pl.when(inner)
     def _():
         lax.fori_loop(half, blocks, forward_far, 0)
 
     pair_on(1)
-    columns(range(4, COLUMN_PIECES))
+    columns(range(2, COLUMN_PIECES))
 
     @pl.when(inner)
     def _():
@@ -354,8 +399,7 @@
     def compute(block, turn):
         step = step_of(turn)
 
-        @pl.when(step == 0)
-        def _():
+        if turn == 0:
             own_piece(block).wait()
 
         for other in range(2):
@@ -366,20 +410,13 @@
             right = jnp.concatenate([w_ref[block, p, span, :] for p in range(3)], axis=1)
             value = jnp.dot(tok_ref[slot, :, span], right, preferred_element_type=jnp.float32)
 
-            @pl.when(step == 0)
-            def _():
-                acc_ref[slot] = value
-
-            @pl.when(step != 0)
-            def _():
-                acc_ref[slot] = acc_ref[slot] + value
-
+            acc_ref[slot] = value if turn == 0 else acc_ref[slot] + value
             return carry
 
         lax.fori_loop(0, 4, one, 0)
 
-        @pl.when(turn == depth - 1)
-        def _():
+        if turn == depth - 1:
+
             def put(slot, carry):
                 proj_ref[slot] = acc_ref[slot].astype(proj_ref.dtype)
                 return carry
@@ -488,7 +525,7 @@
     def combine(block):
         for copy in share_waits(block):
             copy.wait_recv()
-        rates = mode_ref[:, chan(block)]
+        rates = mode_ref[block]
         reach = split(reach_ref[block])
 
         def segment(slot, carry):
@@ -580,17 +617,15 @@
             forward_slot(block, 1)
 
         compute(block, 0)
+        compute(block, 1)
         for turn in range(2, depth - 1):
             forward_slot(block, turn)
-        compute(block, 1)
+            compute(block, turn)
 
         @pl.when(block > 0)
         def _():
             combine(block - 1)
             send_mix(block - 1)
-
-        for turn in range(2, depth - 1):
-            compute(block, turn)
 
         @pl.when(block > 1)
         def _():
@@ -699,14 +734,15 @@
     lax.fori_loop(0, blocks, finish, 0)
 
 
-def hyena(own, w3, w_out, taps, lags, leave, reach, fade, skip, by_mode, width):
+def hyena(own, w3, w_out, taps, decay, residue, skip, width):
     size, n_tp = lax.axis_size("seq"), lax.axis_size("tp")
     line, depth = size // 2, size // 4
     count = own.shape[0]
     chans = w3.shape[2] // 4
     lanes = min(BLOCK, chans)
     blocks = chans // lanes
-    order = by_mode.shape[0]
+    order = decay.shape[0]
+    tile = lanes // width
     tall = HALO + count
     out_cols = w_out.shape[1] // n_tp
     anywhere = pl.BlockSpec(memory_space=pl.ANY)
@@ -722,14 +758,19 @@
             jax.ShapeDtypeStruct((count, out_cols), jnp.bfloat16),
             jax.ShapeDtypeStruct((n_tp - 1, w_out.shape[0], out_cols), w_out.dtype),
         ],
-        in_specs=[anywhere] * 3 + [near] * 7,
+        in_specs=[anywhere] * 3 + [near] * 4,
         out_specs=[near, anywhere],
         scratch_shapes=[
+            pltpu.VMEM((blocks * tile, SUB), jnp.float32),
+            pltpu.VMEM((blocks * tile * order, SUB), jnp.float32),
+            pltpu.VMEM((blocks, count, tile * order), jnp.float32),
+            pltpu.VMEM((blocks * tile * order, lanes), jnp.float32),
+            pltpu.VMEM((blocks, order, lanes), jnp.float32),
             pltpu.VMEM((4, tall, own.shape[1]), own.dtype),
             pltpu.VMEM((blocks, 3, own.shape[1], lanes), w3.dtype),
             pltpu.VMEM((4, tall, 3 * lanes), jnp.float32),
             pltpu.VMEM((4, tall, 3 * lanes), jnp.bfloat16),
-            pltpu.VMEM((lanes // width * SUB, SUB), jnp.bfloat16),
+            pltpu.VMEM((tile * SUB, SUB), jnp.bfloat16),
             pltpu.VMEM((4, count, lanes), jnp.float32),
             pltpu.VMEM((4, count, lanes), jnp.float32),
             pltpu.VMEM((blocks, depth, 4, order, lanes), jnp.float32),
@@ -742,43 +783,13 @@
             collective_id=0, has_side_effects=True, vmem_limit_bytes=60 << 20
         ),
         name="hyena",
-    )(own, w3, w_out, taps, lags, leave, reach, fade, skip, by_mode)[0]
+    )(own, w3, w_out, taps, decay, residue, skip)[0]
 
 
 def shards(tokens, w_in, short_taps, decay_rate, residue, skip_gain, w_out):
-    count = tokens.shape[0]
-    all_chans = w_in.shape[2]
-    width = all_chans // decay_rate.shape[0]
-    z, x, core, depth = place()
-    role = 2 * lax.rem(z, 2) + core
-    by_mode = jnp.repeat(decay_rate.T, width, axis=1)
-
-    def own(array, axis):
-        share = array.shape[axis] // 4
-        return lax.dynamic_slice_in_dim(array, role * share, share, axis)
-
-    decay_rate, residue = own(decay_rate, 0), own(residue, 0)
-    groups, order = decay_rate.shape
-    lanes = min(BLOCK, all_chans // 4)
-    modes = lanes // width * order
-    weight_mode = residue * jnp.sqrt(2.0 * decay_rate / order)
-    offsets = jnp.arange(SUB, dtype=jnp.float32)
-    back = (-jnp.arange(SUB) % SUB).astype(jnp.float32)
-    lags = jnp.einsum(
-        "gm,gmd->gd",
-        weight_mode,
-        jnp.exp(-decay_rate[:, :, None] * back[None, None, :]),
-        precision=HIGHEST,
-    )
-    rate = decay_rate.reshape(groups * order)
-    leave = jnp.exp(-rate[:, None] * (SUB - 1.0 - offsets[None, :]))
-    fade = jnp.exp(-rate * SUB)[:, None]
-    positions = jnp.arange(count, dtype=jnp.float32)
-    rate = rate.reshape(-1, 1, modes)
-    reach = weight_mode.reshape(-1, 1, modes) * jnp.exp(-rate * (positions[None, :, None] + 1.0))
     return hyena(
-        tokens, w_in.transpose(1, 0, 2), w_out, short_taps, lags, leave, reach, fade,
-        skip_gain[None], by_mode, width,
+        tokens, w_in.transpose(1, 0, 2), w_out, short_taps, decay_rate.T, residue.T,
+        skip_gain[None], w_in.shape[2] // decay_rate.shape[0],
     )
 
 

time: 250 us -> 229 us (0.916)
  Pallas kernels: 239 us -> 226 us
  local copies, waits for them, and re-layouts: 6.9 us -> 3.16 us
  other arithmetic: 2.88 us -> 0 us
    pallas_call x1, Pallas kernels: 239 us -> 226 us  [hyena(): pl.pallas_call(functools.partial(hyena_kernel, width), out_shape=[jax.Sha...]
where the time goes in v4:
time: 229 us
  Pallas kernels  226 us (99%)
  local copies, waits for them, and re-layouts  3.16 us (1%)
    pallas_call x1, Pallas kernels, hyena(): pl.pallas_call(functools.partial(hyena_kernel, width), out_shape=[jax.Sha...  226 us

profile of v4, /device:TPU:0, one launch (start us, length us, event | category | flops | bytes accessed | tf_op | source)
XLA Modules:
  0.0 229.3 jit_solution(14501687728718341066)
XLA Ops:
  0.0 226.1 %hyena.1 = (bf16[512,2048]{1,0:T(8,128)(2,1)}, bf16[1,2048,2048]{2,1,0:T(8,128)(2,1)}) custom-call(bf16[512,4096]{1,0:T(8,128)(2,1)} %own_ref.1, bf16[3,256,2048]{2,1,0:T(8,128)(2,1)} %bitcast.4, bf16[2048,4096]{1,0:T(8,128)(2,1)} %out_ref.1, f32[3,3,2048]{2,1,0:T(4,128)} %taps_ref.1, f32[16,128]{1,0:T(8,128)} %bitcast.5, f32[16,128]{1,0:T(8,128)} %bitcast.6, ...), custom_call_target="tpu_custom_call" | custom-call | tf_op jit(solution)/shard_map/hyena/pallas_call | solution.py:755
  226.1 3.2 %copy.9 = bf16[512,2048]{1,0:T(8,128)(2,1)} copy(bf16[512,2048]{1,0:T(8,128)(2,1)} %get-tuple-element.6) | data formatting | bytes 4194304

commit v5 on v4

--- a/solution.py
+++ b/solution.py
@@ -112,7 +112,7 @@
     width,
     own_ref, w3_ref, out_ref, taps_ref, decay_ref, residue_ref, skip_ref,
     mixed_ref, wo_ref,
-    lags_ref, leave_ref, reach_ref, fade_ref, mode_ref, tok_ref, w_ref, acc_ref, proj_ref, toep_ref, query_ref, base_ref, all_ref, mix_ref, full_ref, total_ref,
+    lags_ref, leave_ref, reach_ref, fade_ref, mode_ref, tok_ref, w_ref, acc_ref, proj_ref, toep_ref, query_ref, base_ref, all_ref, mix_ref, full_ref, total_ref, keep_ref,
     local_sems, own_sems,
     line_send, line_recv, pass_send, pass_recv, pair_send, pair_recv,
     tp_send, tp_recv, core_send, core_recv, early_send, early_recv,
@@ -322,6 +322,20 @@
 
     early = begin(own_ref, tok_ref.at[own_slot, body], early_send, early_recv, twin)
     taken.start()
+    chans = blocks * lanes
+
+    def role_rows(slot):
+        return pl.ds(slot * chans, chans)
+
+    kept = [
+        pltpu.make_async_copy(
+            out_ref.at[role_rows(slot), out_span(part)], keep_ref.at[slot], local_sems.at[1 + slot]
+        )
+        for slot in range(4)
+    ]
+    for copy in kept:
+        copy.start()
+    total_ref[...] = jnp.zeros_like(total_ref)
     twins, across = [], {}
 
     def to_twin(which, piece, d):
@@ -376,6 +390,8 @@
     forward_slot(0, 1)
     tokens_on(1)
     taken.wait()
+    for copy in kept:
+        copy.wait()
     for copy in [early] + twins:
         copy.wait_recv()
     for p in range(2):
@@ -601,12 +617,43 @@
             for across_copy in overs(block, n + 1):
                 across_copy.start()
 
+    strip = min(4 * SUB, out_cols)
+
+    def project(block, parts, store=None):
+        pairs = [(d, slot) for d in parts for slot in range(4)]
+        left = jnp.concatenate([full_ref[d, block, slot] for d, slot in pairs], axis=1)
+        span = pl.ds(pl.multiple_of(block * lanes, lanes), lanes)
+
+        def one(n, carry):
+            where = pl.ds(pl.multiple_of(n * strip, strip), strip)
+            right = jnp.concatenate(
+                [
+                    tok_ref[slot, span, pl.ds(pl.multiple_of(d * out_cols + n * strip, strip), strip)]
+                    if d else keep_ref[slot, span, where]
+                    for d, slot in pairs
+                ],
+                axis=0,
+            )
+            value = total_ref[:, where] + jnp.dot(left, right, preferred_element_type=jnp.float32)
+            if store is None:
+                total_ref[:, where] = value
+            else:
+                store[:, where] = value.astype(store.dtype)
+            return carry
+
+        lax.fori_loop(0, out_cols // strip, one, 0)
+
+    def project_far(block, store=None):
+        for copy in over_waits(block):
+            copy.wait_recv()
+        project(block, range(1, n_tp), store)
+
     def stage(block, carry):
         @pl.when(block > 0)
         def _():
+            prepare(block - 1)
             forward_slot(block, 0)
             compute(block - 1, depth - 1)
-            prepare(block - 1)
             convolve(block - 1, 0, 4)
             send_states(block - 1)
 
@@ -630,6 +677,7 @@
         @pl.when(block > 1)
         def _():
             send_over(block - 2)
+            project(block - 2, [0])
 
         return carry
 
@@ -639,77 +687,42 @@
         for d in range(1, n_tp):
             moved[d, piece].wait_recv()
             swaps.append(swap(d, piece))
-    compute(blocks - 1, depth - 1)
-    if blocks > 1:
-        send_over(blocks - 2)
-    loads = []
-
-    def load(source, slot, d):
-        chans = blocks * lanes
-        copy = pltpu.make_async_copy(
-            source, tok_ref.at[slot, pl.ds(0, chans), pl.ds(d * out_cols, out_cols)],
-            local_sems.at[1 + 4 * d + slot],
-        )
-        copy.start()
-        loads.append(copy)
-
-    def role_rows(slot):
-        return pl.ds(slot * blocks * lanes, blocks * lanes)
-
+    last = blocks - 1
+    prepare(last)
+    compute(last, depth - 1)
+    if last:
+        send_over(last - 1)
     inside = twins + list(across.values())
     for copy in inside:
         copy.wait_send()
-    for slot in range(4):
-        load(out_ref.at[role_rows(slot), out_span(part)], slot, 0)
-    prepare(blocks - 1)
-    convolve(blocks - 1, 0, 4)
-    send_states(blocks - 1)
     for copy in swaps:
         copy.wait_recv()
-    for d in range(1, n_tp):
-        for slot in range(4):
-            load(wo_ref.at[d - 1, role_rows(slot)], slot, d)
+    loads = [
+        pltpu.make_async_copy(
+            wo_ref.at[d - 1, role_rows(slot)],
+            tok_ref.at[slot, pl.ds(0, chans), pl.ds(d * out_cols, out_cols)],
+            local_sems.at[1 + 4 * d + slot],
+        )
+        for d in range(1, n_tp)
+        for slot in range(4)
+    ]
+    for copy in loads:
+        copy.start()
+    convolve(last, 0, 4)
+    send_states(last)
+    if last:
+        project(last - 1, [0])
+    combine(last)
+    send_mix(last)
     for copy in loads:
         copy.wait()
-    strip = min(4 * SUB, out_cols)
-
-    def project(block, carry):
-        for copy in over_waits(block):
-            copy.wait_recv()
-        pairs = [(d, slot) for d in range(n_tp) for slot in range(4)]
-        left = jnp.concatenate([full_ref[d, block, slot] for d, slot in pairs], axis=1)
-        span = pl.ds(pl.multiple_of(block * lanes, lanes), lanes)
-
-        def one(n, carry):
-            right = jnp.concatenate(
-                [
-                    tok_ref[slot, span, pl.ds(pl.multiple_of(d * out_cols + n * strip, strip), strip)]
-                    for d, slot in pairs
-                ],
-                axis=0,
-            )
-            value = jnp.dot(left, right, preferred_element_type=jnp.float32)
-            where = pl.ds(pl.multiple_of(n * strip, strip), strip)
-
-            @pl.when(block > 0)
-            def _():
-                total_ref[:, where] = total_ref[:, where] + value
-
-            @pl.when(block == 0)
-            def _():
-                total_ref[:, where] = value
-
-            return carry
-
-        lax.fori_loop(0, out_cols // strip, one, 0)
-        return carry
-
-    lax.fori_loop(0, half, project, 0)
-    combine(blocks - 1)
-    send_mix(blocks - 1)
-    send_over(blocks - 1)
-    lax.fori_loop(half, blocks, project, 0)
-    mixed_ref[...] = total_ref[...].astype(mixed_ref.dtype)
+    for block in range(min(last, 2)):
+        project_far(block)
+    send_over(last)
+    project(last, [0])
+    for block in range(min(last, 2), last):
+        project_far(block)
+    project_far(last, mixed_ref)
     for copy in started:
         if all(copy is not other for other in inside):
             copy.wait_send()
@@ -777,10 +790,11 @@
             pltpu.VMEM((blocks, 4, count, lanes), jnp.bfloat16),
             pltpu.VMEM((n_tp, blocks, 4, count, lanes), jnp.bfloat16),
             pltpu.VMEM((count, out_cols), jnp.float32),
+            pltpu.VMEM((4, blocks * lanes, out_cols), w_out.dtype),
         ]
         + [pltpu.SemaphoreType.DMA(n if isinstance(n, tuple) else (n,) if n else ()) for n in counts],
         compiler_params=pltpu.CompilerParams(
-            collective_id=0, has_side_effects=True, vmem_limit_bytes=60 << 20
+            collective_id=0, has_side_effects=True, vmem_limit_bytes=61 << 20
         ),
         name="hyena",
     )(own, w3, w_out, taps, decay, residue, skip)[0]

time: 229 us -> 226 us (0.987)
  Pallas kernels: 226 us -> 223 us
    pallas_call x1, Pallas kernels: 226 us -> 223 us  [hyena(): pl.pallas_call(functools.partial(hyena_kernel, width), out_shape=[jax.Sha...]
where the time goes in v5:
time: 226 us
  Pallas kernels  223 us (99%)
  local copies, waits for them, and re-layouts  3.16 us (1%)
    pallas_call x1, Pallas kernels, hyena(): pl.pallas_call(functools.partial(hyena_kernel, width), out_shape=[jax.Sha...  223 us

profile of v5, /device:TPU:0, one launch (start us, length us, event | category | flops | bytes accessed | tf_op | source)
XLA Modules:
  0.0 225.9 jit_solution(15614320330878646417)
XLA Ops:
  0.0 222.8 %hyena.1 = (bf16[512,2048]{1,0:T(8,128)(2,1)}, bf16[1,2048,2048]{2,1,0:T(8,128)(2,1)}) custom-call(bf16[512,4096]{1,0:T(8,128)(2,1)} %own_ref.1, bf16[3,256,2048]{2,1,0:T(8,128)(2,1)} %bitcast.4, bf16[2048,4096]{1,0:T(8,128)(2,1)} %out_ref.1, f32[3,3,2048]{2,1,0:T(4,128)} %taps_ref.1, f32[16,128]{1,0:T(8,128)} %bitcast.5, f32[16,128]{1,0:T(8,128)} %bitcast.6, ...), custom_call_target="tpu_custom_call" | custom-call | tf_op jit(solution)/shard_map/hyena/pallas_call | solution.py:768
  222.8 3.2 %copy.9 = bf16[512,2048]{1,0:T(8,128)(2,1)} copy(bf16[512,2048]{1,0:T(8,128)(2,1)} %get-tuple-element.6) | data formatting | bytes 4194304

commit v6 on v5

--- a/solution.py
+++ b/solution.py
@@ -10,6 +10,7 @@
 SUB = 128
 BLOCK = 128
 COLUMN_PIECES = 8
+PIECES = 4
 HALO = 16
 MESH = pl.DeviceIdType.MESH
 
@@ -142,10 +143,10 @@
     tps = [{"tp": lax.rem(part + d, n_tp)} for d in range(1, n_tp)]
     greet([{"seq": lax.rem(mine + d, size)} for d in range(1, size)] + tps)
 
-    cols = own_ref.shape[1] // (2 * n_tp)
+    cols = own_ref.shape[1] // (PIECES * n_tp)
 
     def band(which, piece):
-        return pl.ds(pl.multiple_of((2 * which + piece) * cols, cols), cols)
+        return pl.ds(pl.multiple_of((PIECES * which + piece) * cols, cols), cols)
 
     own_slot, mate_slot = 2 * parity + core, 2 * (1 - parity) + core
     body = pl.ds(HALO, count)
@@ -302,8 +303,8 @@
         issue_step(block, depth - 1)
         return carry
 
-    paired = [to_pair(0), to_pair(1)]
-    columns(range(2))
+    paired = [to_pair(piece) for piece in range(PIECES)]
+    columns(range(1))
     lax.fori_loop(0, blocks, begin_own, 0)
 
     @pl.when(leads)
@@ -340,14 +341,14 @@
 
     def to_twin(which, piece, d):
         where = tok_ref.at[mate_slot, body, band(which, piece)]
-        slot = 2 * d + piece
+        slot = PIECES * d + piece
         twins.append(begin(where, where, core_send.at[slot], core_recv.at[slot], twin))
 
     def pair_on(piece):
         paired[piece].wait_recv()
         where = tok_ref.at[mate_slot, body, band(part, piece)]
         for d in range(1, n_tp):
-            slot = 2 * (d - 1) + piece
+            slot = PIECES * (d - 1) + piece
             across[d, piece] = begin(
                 where, where, tp_send.at[slot], tp_recv.at[slot], tps[d - 1]
             )
@@ -363,14 +364,16 @@
     def _():
         lax.fori_loop(0, half, forward_far, 0)
 
-    pair_on(0)
+    for piece in range(PIECES // 2):
+        pair_on(piece)
 
     @pl.when(inner)
     def _():
         lax.fori_loop(half, blocks, forward_far, 0)
 
-    pair_on(1)
-    columns(range(2, COLUMN_PIECES))
+    for piece in range(PIECES // 2, PIECES):
+        pair_on(piece)
+    columns(range(1, COLUMN_PIECES))
 
     @pl.when(inner)
     def _():
@@ -385,10 +388,12 @@
             across[d, piece].wait_recv()
             to_twin(lax.rem(part - d + n_tp, n_tp), piece, d)
 
-    tokens_on(0)
+    for piece in range(PIECES // 2):
+        tokens_on(piece)
     forward_slot(0, 0)
     forward_slot(0, 1)
-    tokens_on(1)
+    for piece in range(PIECES // 2, PIECES):
+        tokens_on(piece)
     taken.wait()
     for copy in kept:
         copy.wait()
@@ -761,7 +766,7 @@
     anywhere = pl.BlockSpec(memory_space=pl.ANY)
     near = pl.BlockSpec(memory_space=pltpu.VMEM)
     counts = (
-        [1 + 4 * n_tp, blocks] + [(blocks, line)] * 4 + [2, 2] + [2 * n_tp] * 4 + [0, 0]
+        [1 + 4 * n_tp, blocks] + [(blocks, line)] * 4 + [PIECES, PIECES] + [PIECES * n_tp] * 4 + [0, 0]
         + [COLUMN_PIECES * n_tp] * 4 + [4, 2]
         + [(blocks, depth - 1)] * 2 + [(blocks, 3)] * 2 + [(blocks, 4 * n_tp)] * 2
     )

time: 226 us -> 226 us (level)
  no operation moved by 1% of the time
where the time goes in v6:
time: 226 us
  Pallas kernels  223 us (99%)
  local copies, waits for them, and re-layouts  3.16 us (1%)
    pallas_call x1, Pallas kernels, hyena(): pl.pallas_call(functools.partial(hyena_kernel, width), out_shape=[jax.Sha...  223 us

profile of v6, /device:TPU:0, one launch (start us, length us, event | category | flops | bytes accessed | tf_op | source)
XLA Modules:
  0.0 226.1 jit_solution(15691979663723547031)
XLA Ops:
  0.0 223.0 %hyena.1 = (bf16[512,2048]{1,0:T(8,128)(2,1)}, bf16[1,2048,2048]{2,1,0:T(8,128)(2,1)}) custom-call(bf16[512,4096]{1,0:T(8,128)(2,1)} %own_ref.1, bf16[3,256,2048]{2,1,0:T(8,128)(2,1)} %bitcast.4, bf16[2048,4096]{1,0:T(8,128)(2,1)} %out_ref.1, f32[3,3,2048]{2,1,0:T(4,128)} %taps_ref.1, f32[16,128]{1,0:T(8,128)} %bitcast.5, f32[16,128]{1,0:T(8,128)} %bitcast.6, ...), custom_call_target="tpu_custom_call" | custom-call | tf_op jit(solution)/shard_map/hyena/pallas_call | solution.py:773
  223.0 3.2 %copy.9 = bf16[512,2048]{1,0:T(8,128)(2,1)} copy(bf16[512,2048]{1,0:T(8,128)(2,1)} %get-tuple-element.6) | data formatting | bytes 4194304
